TPU v7x, 32 devices: a whole 2x2x4 slice. The times are simulated.
32 devices in a mesh: blk: 8 (over y, x, core), virt: 4 (over z).
Axes of the slice: x: 2, y: 2, z: 4, core: 2. Of those that a mesh axis runs over, the one named last changes fastest.
Arguments:
- integral_tiles: bfloat16 [4, 1024, 128, 128], P('virt', 'blk'), may hold values from -0.1875 to 0.1875
- tile_panel: int32 [4, 1024, 1], P('virt', 'blk'), may hold values from 0 to 7; in each aligned block of 128 rows (0 to 127, 128 to 255, ..., all dimensions but the last counted through in order) at most 32 rows name the same one
- tile_row: int32 [4, 1024], P('virt', 'blk'), may hold values from 0 to 11
- tile_col: int32 [4, 1024], P('virt', 'blk'), may hold values from 0 to 7
- green_factor: float32 [1024, 8192], P('blk'), may hold values from -6 to 6
- window_start: int32 [1], replicated, may hold values from 0 to 7168
Outputs:
- response: float32 [12288, 1536], P(('blk', 'virt'))
Inputs may be any that keep to these rules, and one draw needn't show every extreme that they name: `tile_panel`: within the tiles of one device, at most 32 name the same panel, and some device has exactly 32 for one panel.
All inputs are finite; a program needn't handle non-finite values.
Results may differ from a plain program's by a relative error of at most 0.0019.
Values may be sent and summed in bfloat16 or wider, within the bound.
No kernel may reach another device: no remote copies, remote signals or barrier semaphores. Data moves between devices by JAX's collectives and lax.ppermute only.
A program may use at most 128 MiB of HBM per device.

v0:
```python
import functools
import math

import jax
import jax.numpy as jnp
from jax import lax
from jax.experimental import pallas as pl
from jax.experimental.pallas import tpu as pltpu
from jax.sharding import PartitionSpec as P


NOCC = 1024
STOPS = 8
PANEL = 1536
LABEL_ROWS = 16
AXES = ("blk", "virt")


def offset_order(count):
    def key(offset):
        chip = offset // 2
        return (bin(chip).count("1") or count, offset % 2, chip)

    return sorted(range(count), key=key)


def partner(block, offset, count):
    return block ^ offset if count & (count - 1) == 0 else (block + offset) % count


def place_of(panel, slab, virt_count):
    return (2 * (panel // 2) + slab % 2) * virt_count + 2 * (slab // 2) + panel % 2


def pack_kernel(count, slots, order, panel_s, panel_row, row_row, column_row, tiles, *rest):
    made, rest = rest[:count], rest[count:]
    held, label_rows, label_blocks, slot_tile, used, in_sem, out_sem, label_sem = rest
    tile_count, edge = held.shape[0], held.shape[1]
    parts = in_sem.shape[0]
    per_part = tile_count // parts
    me = lax.axis_index("blk")
    loads = [
        pltpu.make_async_copy(
            tiles.at[pl.ds(part * per_part, per_part)],
            held.at[pl.ds(part * per_part, per_part)],
            in_sem.at[part],
        )
        for part in range(parts)
    ]
    for load in loads:
        load.start()
    for panel in range(count):
        used[panel] = 0

    @pl.loop(0, tile_count)
    def _(at):
        panel = panel_s[at]
        slot = used[panel]
        slot_tile[panel * slots + slot] = at
        used[panel] = slot + 1

    panels = panel_row[...]
    square = (tile_count, tile_count)
    one_hot = (panels == lax.broadcasted_iota(jnp.int32, (max(count, 8), tile_count), 0)).astype(jnp.float32)
    earlier = lax.broadcasted_iota(jnp.int32, square, 0) < lax.broadcasted_iota(jnp.int32, square, 1)
    before = jnp.dot(
        one_hot.astype(jnp.bfloat16),
        earlier.astype(jnp.float32).astype(jnp.bfloat16),
        preferred_element_type=jnp.float32,
    )
    rank = jnp.sum(before * one_hot, axis=0, keepdims=True)
    at_slot = jnp.broadcast_to(rank, square).T == lax.broadcasted_iota(jnp.int32, square, 1).astype(jnp.float32)
    code = row_row[...] * STOPS + column_row[...]
    codes = one_hot * (code.astype(jnp.float32) + 1.0)
    label_rows[...] = (
        jnp.dot(
            codes.astype(jnp.bfloat16),
            at_slot.astype(jnp.float32).astype(jnp.bfloat16),
            preferred_element_type=jnp.float32,
        )
        - 1.0
    )
    label_copies = []
    for at, offset in enumerate(order):
        row = label_rows[pl.ds(partner(me, offset, count), 1), :]
        label_blocks[at] = jnp.broadcast_to(row, (LABEL_ROWS, tile_count)).astype(jnp.bfloat16)
        target = made[at].at[pl.ds(slots * edge, LABEL_ROWS)]
        label_copies.append(pltpu.make_async_copy(label_blocks.at[at], target, label_sem.at[at]))
        label_copies[-1].start()
    for load in loads:
        load.wait()
    for offset, target in zip(order, made):
        panel = partner(me, offset, count)

        @pl.loop(0, used[panel])
        def _(slot):
            pltpu.make_async_copy(
                held.at[slot_tile[panel * slots + slot]],
                target.at[pl.ds(pl.multiple_of(slot * edge, edge), edge)],
                out_sem,
            ).start()

    for copy in label_copies:
        copy.wait()
    pltpu.make_async_copy(tiles, held, out_sem).wait()


def pack(tiles, tile_panel, tile_row, tile_col, count, slots, order):
    tile_count, edge = tiles.shape[0], tiles.shape[1]
    shapes = [jax.ShapeDtypeStruct((slots * edge + LABEL_ROWS, edge), tiles.dtype)] * count
    return pl.pallas_call(
        functools.partial(pack_kernel, count, slots, order),
        out_shape=shapes,
        in_specs=[
            pl.BlockSpec(memory_space=pltpu.SMEM),
            pl.BlockSpec(memory_space=pltpu.VMEM),
            pl.BlockSpec(memory_space=pltpu.VMEM),
            pl.BlockSpec(memory_space=pltpu.VMEM),
            pl.BlockSpec(memory_space=pl.ANY),
        ],
        out_specs=[pl.BlockSpec(memory_space=pl.ANY)] * count,
        scratch_shapes=[
            pltpu.VMEM(tiles.shape, tiles.dtype),
            pltpu.VMEM((max(count, 8), tile_count), jnp.float32),
            pltpu.VMEM((count, LABEL_ROWS, tile_count), jnp.bfloat16),
            pltpu.SMEM((count * slots,), jnp.int32),
            pltpu.SMEM((count,), jnp.int32),
            pltpu.SemaphoreType.DMA((4,)),
            pltpu.SemaphoreType.DMA,
            pltpu.SemaphoreType.DMA((count,)),
        ],
        name="pack",
    )(tile_panel, tile_panel.reshape(1, tile_count), tile_row, tile_col, tiles)


def couple_kernel(count, slots, edge, *rest):
    messages, rest = rest[:count], rest[count:]
    coarse, fine, rest = rest[:STOPS], rest[STOPS : 2 * STOPS], rest[2 * STOPS :]
    result, held, basis, basis_rest, dense, made, rest = *rest[:6], rest[6:]
    label_blocks, label_rows, labels, tile_sem, basis_sem, label_sem, out_sem = rest
    core = lax.axis_index("blk") % 2
    loads = []
    for at in range(STOPS // 2):
        for half, stop in ((0, 2 * at + core), (STOPS // 2, 2 * at + 1 - core)):
            rows = pl.ds(pl.multiple_of(stop * edge, edge), edge)
            for ref, target in ((coarse[half + at], basis), (fine[half + at], basis_rest)):
                loads.append(pltpu.make_async_copy(ref, target.at[rows], basis_sem.at[len(loads)]))
    height = slots * edge
    label_loads = [
        pltpu.make_async_copy(ref.at[pl.ds(height, LABEL_ROWS)], label_blocks.at[at], label_sem.at[at])
        for at, ref in enumerate(messages)
    ]
    copies = [
        pltpu.make_async_copy(ref.at[pl.ds(0, height)], held.at[at], tile_sem.at[at]) for at, ref in enumerate(messages)
    ]
    for copy in label_loads + copies + loads:
        copy.start()
    dense[...] = jnp.zeros_like(dense)
    for at, copy in enumerate(label_loads):
        copy.wait()
        label_rows[pl.ds(at, 1), :] = label_blocks[at].astype(jnp.float32)[:1].astype(jnp.int32)
    copy = pltpu.make_async_copy(label_rows, labels, out_sem)
    copy.start()
    copy.wait()
    for at, copy in enumerate(copies):
        copy.wait()

        @pl.loop(0, slots)
        def _(slot):
            label = labels[at, slot]

            @pl.when(label >= 0)
            def _():
                rows = pl.ds(pl.multiple_of(label // STOPS * edge, edge), edge)
                columns = pl.ds(pl.multiple_of(label % STOPS * edge, edge), edge)
                tile = held[at, pl.ds(pl.multiple_of(slot * edge, edge), edge), :]
                dense[rows, columns] += tile.astype(jnp.float32)

    for load in loads:
        load.wait()
    step = PANEL // 4

    @pl.loop(0, 4)
    def _(at):
        rows = pl.ds(pl.multiple_of(at * step, step), step)
        value = dense[rows, :]
        high = value.astype(jnp.bfloat16)
        low = (value - high.astype(jnp.float32)).astype(jnp.bfloat16)
        sums = jnp.dot(high, basis_rest[...], preferred_element_type=jnp.float32)
        sums += jnp.dot(low, basis[...], preferred_element_type=jnp.float32)
        sums += jnp.dot(high, basis[...], preferred_element_type=jnp.float32)
        made[rows, :] = sums.astype(jnp.bfloat16)
        pltpu.make_async_copy(made.at[rows], result.at[rows], out_sem).start()

    pltpu.make_async_copy(made, result, out_sem).wait()


def couple(messages, coarse, fine, count, slots, edge):
    operands = [*messages, *coarse, *fine]
    return pl.pallas_call(
        functools.partial(couple_kernel, count, slots, edge),
        out_shape=jax.ShapeDtypeStruct((PANEL, NOCC), jnp.bfloat16),
        in_specs=[pl.BlockSpec(memory_space=pl.ANY)] * len(operands),
        out_specs=pl.BlockSpec(memory_space=pl.ANY),
        scratch_shapes=[
            pltpu.VMEM((count, slots * edge, edge), jnp.bfloat16),
            pltpu.VMEM((STOPS * edge, NOCC), jnp.bfloat16),
            pltpu.VMEM((STOPS * edge, NOCC), jnp.bfloat16),
            pltpu.VMEM((PANEL, STOPS * edge), jnp.float32),
            pltpu.VMEM((PANEL, NOCC), jnp.bfloat16),
            pltpu.VMEM((count, LABEL_ROWS, edge), jnp.bfloat16),
            pltpu.VMEM((count, edge), jnp.int32),
            pltpu.SMEM((count, edge), jnp.int32),
            pltpu.SemaphoreType.DMA((count,)),
            pltpu.SemaphoreType.DMA((2 * STOPS,)),
            pltpu.SemaphoreType.DMA((count,)),
            pltpu.SemaphoreType.DMA,
        ],
        compiler_params=pltpu.CompilerParams(vmem_limit_bytes=36 * 1024 * 1024),
        name="couple",
    )(*operands)


STEPS = 32000.0


def coded(value):
    top = jnp.max(jnp.abs(value), axis=1, keepdims=True)
    scale_code = jnp.ceil(jnp.log2(jnp.maximum(top, 1e-30)) * 256.0)
    steps = jnp.round(value * (STEPS / jnp.exp2(scale_code / 256.0)))
    whole = jnp.concatenate([steps, jnp.broadcast_to(scale_code, (value.shape[0], 128))], axis=1)
    return whole.astype(jnp.int32).astype(jnp.int16)


def decoded(code, width):
    number = code.astype(jnp.int32).astype(jnp.float32)
    return number[:, :width] * (jnp.exp2(number[:, width : width + 1] / 256.0) / STEPS)


def upper_blocks(count):
    return [(i, j) for i in range(count) for j in range(i, count)]


def rows_times_rows(left, right):
    return lax.dot_general(left, right, (((1,), (1,)), ((), ())), preferred_element_type=jnp.float32)


def load_halves(theirs, near, far, sems):
    half = near.shape[0]
    core = lax.axis_index("blk") % 2
    copies = []
    for at, (target, which) in enumerate(((near, core), (far, 1 - core))):
        rows = pl.ds(pl.multiple_of(which * half, half), half)
        copies.append(pltpu.make_async_copy(theirs.at[rows], target, sems.at[at]))
        copies[-1].start()
    return copies


def message_rows(near, message, piece):
    turn = (lax.axis_index("virt") // 2 + message) % 2
    return near[pl.ds(pl.multiple_of(turn * piece, piece), piece), :]


def own_join_kernel(piece, mine, between, *rest):
    acrosses, corners, (near, far, sems) = rest[:2], rest[2:4], rest[4:]
    copies = load_halves(mine, near, far, sems)
    copies[0].wait()
    between[...] = rows_times_rows(near[:piece, :], near[piece:, :])
    for message in range(2):
        rows = message_rows(near, message, piece)
        corners[message][...] = rows_times_rows(rows, rows)
    copies[1].wait()
    for message in range(2):
        acrosses[message][...] = rows_times_rows(message_rows(near, message, piece), far[...])


def own_join(mine, piece):
    half = mine.shape[0] // 2
    square, wide = (jax.ShapeDtypeStruct((piece, width), jnp.float32) for width in (piece, half))
    return pl.pallas_call(
        functools.partial(own_join_kernel, piece),
        out_shape=[square, wide, wide, square, square],
        in_specs=[pl.BlockSpec(memory_space=pl.ANY)],
        out_specs=[pl.BlockSpec(memory_space=pltpu.VMEM)] * 5,
        scratch_shapes=[
            pltpu.VMEM((half, mine.shape[1]), jnp.bfloat16),
            pltpu.VMEM((half, mine.shape[1]), jnp.bfloat16),
            pltpu.SemaphoreType.DMA((2,)),
        ],
        compiler_params=pltpu.CompilerParams(vmem_limit_bytes=20 * 1024 * 1024),
        name="own_join",
    )(mine)


def first_join_kernel(piece, theirs, between_part, across_part, between, across, near, far, held_b, held_a, sems):
    copies = load_halves(theirs, near, far, sems)
    for at, (ref, target) in enumerate(((between_part, held_b), (across_part, held_a))):
        copies.append(pltpu.make_async_copy(ref, target, sems.at[2 + at]))
        copies[-1].start()
    copies[0].wait()
    copies[2].wait()
    between[...] = (held_b[...] + rows_times_rows(near[:piece, :], near[piece:, :])).astype(jnp.bfloat16)
    copies[1].wait()
    copies[3].wait()
    across[...] = (held_a[...] + rows_times_rows(message_rows(near, 0, piece), far[...])).astype(jnp.bfloat16)


def second_join_kernel(piece, edge, theirs, across_part, *rest):
    corner_parts, (across, *corners), (near, far, held_a, *held_c, sems) = rest[:2], rest[2:5], rest[5:]
    copies = load_halves(theirs, near, far, sems)
    for at, (ref, target) in enumerate(zip((across_part, *corner_parts), (held_a, *held_c))):
        copies.append(pltpu.make_async_copy(ref, target, sems.at[2 + at]))
        copies[-1].start()
    copies[0].wait()
    for message in range(2):
        copies[3 + message].wait()
        rows = message_rows(near, message, piece)
        block = held_c[message][...] + rows_times_rows(rows, rows)
        for at, (i, j) in enumerate(upper_blocks(piece // edge)):
            corners[message][at * edge : (at + 1) * edge, :] = block[
                i * edge : (i + 1) * edge, j * edge : (j + 1) * edge
            ].astype(jnp.bfloat16)
    copies[1].wait()
    copies[2].wait()
    across[...] = (held_a[...] + rows_times_rows(message_rows(near, 1, piece), far[...])).astype(jnp.bfloat16)


def first_join(theirs, between_part, across_part, piece):
    half = theirs.shape[0] // 2
    return pl.pallas_call(
        functools.partial(first_join_kernel, piece),
        out_shape=[
            jax.ShapeDtypeStruct((piece, piece), jnp.bfloat16),
            jax.ShapeDtypeStruct((piece, half), jnp.bfloat16),
        ],
        in_specs=[pl.BlockSpec(memory_space=pl.ANY)] * 3,
        out_specs=[pl.BlockSpec(memory_space=pltpu.VMEM)] * 2,
        scratch_shapes=[
            pltpu.VMEM((half, theirs.shape[1]), jnp.bfloat16),
            pltpu.VMEM((half, theirs.shape[1]), jnp.bfloat16),
            pltpu.VMEM((piece, piece), jnp.float32),
            pltpu.VMEM((piece, half), jnp.float32),
            pltpu.SemaphoreType.DMA((4,)),
        ],
        compiler_params=pltpu.CompilerParams(vmem_limit_bytes=20 * 1024 * 1024),
        name="first_join",
    )(theirs, between_part, across_part)


def second_join(theirs, across_part, corner_part, other_corner_part, piece, edge):
    half = theirs.shape[0] // 2
    packed = (len(upper_blocks(piece // edge)) * edge, edge)
    return pl.pallas_call(
        functools.partial(second_join_kernel, piece, edge),
        out_shape=[
            jax.ShapeDtypeStruct((piece, half), jnp.bfloat16),
            jax.ShapeDtypeStruct(packed, jnp.bfloat16),
            jax.ShapeDtypeStruct(packed, jnp.bfloat16),
        ],
        in_specs=[pl.BlockSpec(memory_space=pl.ANY)] * 4,
        out_specs=[pl.BlockSpec(memory_space=pltpu.VMEM)] * 3,
        scratch_shapes=[
            pltpu.VMEM((half, theirs.shape[1]), jnp.bfloat16),
            pltpu.VMEM((half, theirs.shape[1]), jnp.bfloat16),
            pltpu.VMEM((piece, half), jnp.float32),
            pltpu.VMEM((piece, piece), jnp.float32),
            pltpu.VMEM((piece, piece), jnp.float32),
            pltpu.SemaphoreType.DMA((5,)),
        ],
        compiler_params=pltpu.CompilerParams(vmem_limit_bytes=20 * 1024 * 1024),
        name="second_join",
    )(theirs, across_part, corner_part, other_corner_part)


def assemble_kernel(piece, edge, factor, link, passed, side, other_side, corner, other_corner, result, *rest):
    made, rest = rest[0], rest[1:]
    held, sems, out_sem = rest[:6], rest[6], rest[7]
    half = 2 * piece
    virt = lax.axis_index("virt")
    order = (side, other_side, corner, other_corner, link, passed)
    copies = [pltpu.make_async_copy(ref, target, sems.at[at]) for at, (ref, target) in enumerate(zip(order, held))]
    for copy in copies:
        copy.start()
    side_h, other_side_h, corner_h, other_corner_h, link_h, passed_h = held

    def store(start, value):
        made[:, pl.ds(pl.multiple_of(start, edge), value.shape[1])] = value * factor

    def put(start):
        columns = pl.ds(pl.multiple_of(start, edge), half)
        copy = pltpu.make_async_copy(made.at[:, columns], result.at[:, columns], out_sem)
        copy.start()

    near, far = virt // 2 * half, (1 - virt // 2) * half
    copies[0].wait()
    copies[1].wait()
    store(far, side_h[...].astype(jnp.float32) + other_side_h[...].astype(jnp.float32))
    put(far)
    copies[2].wait()
    copies[3].wait()
    count = piece // edge
    blocks = {}
    for at, place in enumerate(upper_blocks(count)):
        rows = slice(at * edge, (at + 1) * edge)
        blocks[place] = corner_h[rows, :].astype(jnp.float32) + other_corner_h[rows, :].astype(jnp.float32)
    rows = [
        jnp.concatenate([blocks[i, j] if i <= j else blocks[j, i].T for j in range(count)], axis=1)
        for i in range(count)
    ]
    store(near + virt % 2 * piece, jnp.concatenate(rows, axis=0))
    copies[4].wait()
    copies[5].wait()

    @pl.when(virt % 2 == 0)
    def _():
        store(near + piece, link_h[...])

    @pl.when(virt % 2 == 1)
    def _():
        store(near, passed_h[...].astype(jnp.float32).T)

    put(near)
    pltpu.make_async_copy(made, result, out_sem).wait()


def assemble(link, passed, sides, corners, piece, edge, factor):
    operands = (link, passed, *sides, *corners)
    width = 4 * piece
    return pl.pallas_call(
        functools.partial(assemble_kernel, piece, edge, factor),
        out_shape=jax.ShapeDtypeStruct((piece, width), jnp.float32),
        in_specs=[pl.BlockSpec(memory_space=pl.ANY)] * len(operands),
        out_specs=pl.BlockSpec(memory_space=pl.ANY),
        scratch_shapes=[pltpu.VMEM((piece, width), jnp.float32)]
        + [pltpu.VMEM(array.shape, array.dtype) for array in (*sides, *corners, link, passed)]
        + [pltpu.SemaphoreType.DMA((6,)), pltpu.SemaphoreType.DMA],
        compiler_params=pltpu.CompilerParams(vmem_limit_bytes=20 * 1024 * 1024),
        name="assemble",
    )(*operands)


def per_device(integral_tiles, tile_panel, tile_row, tile_col, green_factor, window_start):
    count = lax.axis_size("blk")
    virt_count = lax.axis_size("virt")
    tile_count, edge = integral_tiles.shape[1], integral_tiles.shape[2]
    slots = max(2, 2 * tile_count // count)
    order = offset_order(count)
    middle = STOPS // 2
    everyone = [(block, virt) for block in range(count) for virt in range(virt_count)]

    packed = pack(integral_tiles[0], tile_panel[0, :, 0], tile_row, tile_col, count, slots, order)
    sent = []
    for offset, message in zip(order, packed):
        pairs = [
            (block * virt_count + virt, place_of(partner(block, offset, count), virt, virt_count))
            for block, virt in everyone
        ]
        sent.append(lax.ppermute(message, AXES, pairs))

    window = coded(lax.dynamic_slice_in_dim(green_factor, window_start[0], NOCC, 1))
    own = []
    for at in range(middle):
        pairs = []
        for block, virt in everyone:
            odd = virt % 2
            core = (block - odd) % 2
            panel = (block - odd - core - 2 * at + middle) % count
            pairs.append((block * virt_count + virt, (panel + core) * virt_count + virt))
        own.append(lax.ppermute(window, AXES, pairs))
    swap = [(block, block ^ 1) for block in range(count)]
    other = [lax.ppermute(array, "blk", swap) for array in own]
    coarse, fine = [], []
    for part in own + other:
        part = decoded(part, NOCC)
        top = lax.reduce_precision(part, 8, 7)
        coarse.append(top.astype(jnp.bfloat16))
        fine.append((part - top).astype(jnp.bfloat16))
    total = couple(sent, coarse, fine, count, slots, edge)

    mine = total
    theirs = lax.ppermute(mine, "blk", swap)
    piece = PANEL // virt_count
    between, *parts = own_join(mine, piece)
    between, across = first_join(theirs, between, parts[0], piece)
    other_across, *corners = second_join(theirs, *parts[1:], piece, edge)

    def sent_to(array, message=None, group=None):
        pairs = []
        for block, virt in everyone:
            row = block % 2 * 2 + (0 if message is None else (virt // 2 + message) % 2)
            if group is None or virt // 2 == group:
                pairs.append((block * virt_count + virt, (2 * (block // 2) + virt % 2) * virt_count + row))
        return lax.ppermute(array, AXES, pairs)

    links = [sent_to(between, group=group) for group in range(2)]
    sides = [sent_to(across, 0)]
    for message, corner in enumerate(corners):
        corners[message] = sent_to(corner, message)
    sides.append(sent_to(other_across, 1))
    on = [
        (block * virt_count + virt, block * virt_count + virt + 1)
        for block, virt in everyone
        if virt % 2 == 0
    ]
    link = links[0].astype(jnp.float32) + links[1].astype(jnp.float32)
    passed = lax.ppermute(link.astype(jnp.bfloat16), AXES, on)
    return assemble(link, passed, sides, corners, piece, edge, -1.0 / math.sqrt(virt_count * NOCC))


def solution(mesh):
    return jax.shard_map(
        per_device,
        mesh=mesh,
        in_specs=(
            P("virt", "blk", None, None),
            P("virt", "blk", None),
            P("virt", "blk"),
            P("virt", "blk"),
            P("blk", None),
            P(),
        ),
        out_specs=P(("blk", "virt"), None),
        check_vma=False,
    )
```

profile of v0, /device:TPU:0, one launch (start us, length us, event | category | flops | bytes accessed | tf_op | source)
XLA Modules:
  0.0 188.9 jit_solution(15880890561146093085)
XLA Ops:
  0.7 1.3 abs_reduce_fusion
  2.0 1.3 multiply_round-nearest-even_fusion
  3.5 3.0 %collective-permute-start.8 = (s16[128,1152]{1,0:T(8,128)(2,1)S(1)}, s16[128,1152]{1,0:T(8,128)(2,1)S(1)}, u32[]{:S(2)}, u32[]{:S(2)}) collective-permute-start(s16[128,1152]{1,0:T(8,128)(2,1)S(1)} %fusion), channel_id=1, source_target_pairs={{0,16},{1,13},{2,18},{3,15},{4,20},{5,17},{6,22},{7,19},{8,24},{9,... | collective-permute-start | bytes 884744 | tf_op jit(solution)/shard_map/ppermute | solution.py:469
  6.5 1.4 collective-permute-start.11
  8.0 0.7 collective-permute-start.10
  8.6 0.6 collective-permute-start.9
  9.3 5.0 %pack.1 = (bf16[4112,128]{1,0:T(8,128)(2,1)}, bf16[4112,128]{1,0:T(8,128)(2,1)}, bf16[4112,128]{1,0:T(8,128)(2,1)}, bf16[4112,128]{1,0:T(8,128)(2,1)}, bf16[4112...) custom-call(s32[128]{0:T(128)} %bitcast.8, ...), custom_call_target="tpu_custom_call" | custom-call | tf_op jit(solution)/shard_map/pack/pallas_call | solution.py:111
  14.3 2.5 %collective-permute-start = (bf16[4112,128]{1,0:T(8,128)(2,1)}, bf16[4112,128]{1,0:T(8,128)(2,1)S(1)}, u32[]{:S(2)}, u32[]{:S(2)}) collective-permute-start(bf16[4112,128]{1,0:T(8,128)(2,1)} %get-tuple-element.23), channel_id=1, source_target_pairs={{0,8},{1,12},{2,10},{3,14},{4,9},{5,13},{6,11},{7,15},{8,0},{9,4},... | collective-permute-start | bytes 3158024 | tf_op jit(solution)/shard_map/ppermute | solution.py:458
  16.8 0.5 collective-permute-start.1
  17.5 0.2 fusion.1
  17.6 15.8 %collective-permute-done.9 = s16[128,1152]{1,0:T(8,128)(2,1)S(1)} collective-permute-done((s16[128,1152]{1,0:T(8,128)(2,1)S(1)}, s16[128,1152]{1,0:T(8,128)(2,1)S(1)}, u32[]{:S(2)}, u32[]{:S(2)}) %collective-permute-start.9) | collective-permute-done | bytes 294944 | tf_op jit(solution)/shard_map/ppermute | solution.py:469
  33.5 1.0 collective-permute-start.2
  34.7 0.2 fusion.2
  34.9 1.6 collective-permute-start.3
  36.7 0.2 fusion.3
  36.8 0.4 collective-permute-start.15
  37.4 0.1 fusion.4
  37.6 0.9 collective-permute-done.15
  38.5 0.3 collective-permute-start.14
  38.9 1.2 collective-permute-done.14
  40.1 0.3 collective-permute-start.13
  40.5 1.1 collective-permute-done.13
  41.6 0.3 collective-permute-start.12
  42.4 0.8 collective-permute-done.12
  43.2 2.5 %collective-permute-start.4 = (bf16[4112,128]{1,0:T(8,128)(2,1)S(1)}, bf16[4112,128]{1,0:T(8,128)(2,1)S(1)}, u32[]{:S(2)}, u32[]{:S(2)}) collective-permute-start(bf16[4112,128]{1,0:T(8,128)(2,1)S(1)} %copy-done.3), channel_id=1, source_target_pairs={{0,24},{1,28},{2,26},{3,30},{4,25},{5,29},{6,27},{7,31},{8,16},{9,... | collective-permute-start | bytes 3158024 | tf_op jit(solution)/shard_map/ppermute | solution.py:458
  45.8 31.4 %collective-permute-done.rest_0_ = bf16[4112,128]{1,0:T(8,128)(2,1)S(1)} collective-permute-done((bf16[4112,128]{1,0:T(8,128)(2,1)}, bf16[4112,128]{1,0:T(8,128)(2,1)S(1)}, u32[]{:S(2)}, u32[]{:S(2)}) %collective-permute-start) | collective-permute-done | bytes 1052704 | tf_op jit(solution)/shard_map/ppermute | solution.py:458
  77.2 0.7 collective-permute-start.6
  78.0 9.6 %collective-permute-done.2.rest_2_ = bf16[4112,128]{1,0:T(8,128)(2,1)S(1)} collective-permute-done((bf16[4112,128]{1,0:T(8,128)(2,1)S(1)}, bf16[4112,128]{1,0:T(8,128)(2,1)S(1)}, u32[]{:S(2)}, u32[]{:S(2)}) %collective-permute-start.2) | collective-permute-done | bytes 1052704 | tf_op jit(solution)/shard_map/ppermute | solution.py:458
  87.6 0.1 fusion.8
  87.8 0.1 fusion.7
  88.1 0.1 fusion.5
  88.2 2.2 %collective-permute-done.3.rest_3_ = bf16[4112,128]{1,0:T(8,128)(2,1)S(1)} collective-permute-done((bf16[4112,128]{1,0:T(8,128)(2,1)S(1)}, bf16[4112,128]{1,0:T(8,128)(2,1)S(1)}, u32[]{:S(2)}, u32[]{:S(2)}) %collective-permute-start.3) | collective-permute-done | bytes 1052704 | tf_op jit(solution)/shard_map/ppermute | solution.py:458
  90.5 17.4 %collective-permute-done.4.rest_4_ = bf16[4112,128]{1,0:T(8,128)(2,1)S(1)} collective-permute-done((bf16[4112,128]{1,0:T(8,128)(2,1)S(1)}, bf16[4112,128]{1,0:T(8,128)(2,1)S(1)}, u32[]{:S(2)}, u32[]{:S(2)}) %collective-permute-start.4) | collective-permute-done | bytes 1052704 | tf_op jit(solution)/shard_map/ppermute | solution.py:458
  107.9 4.8 %collective-permute-done.5.rest_5_ = bf16[4112,128]{1,0:T(8,128)(2,1)S(1)} collective-permute-done((bf16[4112,128]{1,0:T(8,128)(2,1)S(1)}, bf16[4112,128]{1,0:T(8,128)(2,1)S(1)}, u32[]{:S(2)}, u32[]{:S(2)}) %collective-permute-start.5) | collective-permute-done | bytes 1052704 | tf_op jit(solution)/shard_map/ppermute | solution.py:458
  112.7 18.5 %couple.1.mine = bf16[1536,1024]{1,0:T(8,128)(2,1)S(1)} custom-call(bf16[4112,128]{1,0:T(8,128)(2,1)S(1)} %collective-permute-done.rest_0_, bf16[4112,128]{1,0:T(8,128)(2,1)S(1)} %collective-permute-done.1.rest_1_, bf16[4112,128]{1,0:T(8,128)(2,1)S(1)} %collective-permute-done.2.rest_2_, bf16[4112,128]{1,0:T(8,128)(2,1)S(1)} %collective-permute-done.3.rest_3_, ...), custom_call_target="tpu_custom_call" | custom-call | tf_op jit(solution)/shard_map/couple/pallas_call | solution.py:200
  131.3 3.1 %own_join.1 = (f32[384,384]{1,0:T(8,128)S(1)}, f32[384,768]{1,0:T(8,128)S(1)}, f32[384,768]{1,0:T(8,128)S(1)}, f32[384,384]{1,0:T(8,128)S(1)}, f32[384,384]{1,0:T(8,128)S(1)}) custom-call(bf16[1536,1024]{1,0:T(8,128)(2,1)S(1)} %couple.1.mine), custom_call_target="tpu_custom_call" | custom-call | tf_op jit(solution)/shard_map/own_join/pallas_call | solution.py:280
  134.4 2.5 %collective-permute-done.16.theirs = bf16[1536,1024]{1,0:T(8,128)(2,1)S(1)} collective-permute-done((bf16[1536,1024]{1,0:T(8,128)(2,1)S(1)}, bf16[1536,1024]{1,0:T(8,128)(2,1)S(1)}, u32[]{:S(2)}, u32[]{:S(2)}) %collective-permute-start.16) | collective-permute-done | bytes 3145760 | tf_op jit(solution)/shard_map/ppermute | solution.py:481
  136.9 2.2 %first_join.1 = (bf16[384,384]{1,0:T(8,128)(2,1)S(1)}, bf16[384,768]{1,0:T(8,128)(2,1)S(1)}) custom-call(bf16[1536,1024]{1,0:T(8,128)(2,1)S(1)} %collective-permute-done.16.theirs, f32[384,384]{1,0:T(8,128)S(1)} %get-tuple-element.31.between_part, f32[384,768]{1,0:T(8,128)S(1)} %get-tuple-element.32.across_part), custom_call_target="tpu_custom_call" | custom-call | tf_op jit(solution)/shard_map/first_join/pallas_call | solution.py:330
  139.2 1.3 collective-permute-start.18
  140.5 0.9 collective-permute-start.17
  141.3 3.0 %second_join.1 = (bf16[384,768]{1,0:T(8,128)(2,1)S(1)}, bf16[768,128]{1,0:T(8,128)(2,1)S(1)}, bf16[768,128]{1,0:T(8,128)(2,1)S(1)}) custom-call(bf16[1536,1024]{1,0:T(8,128)(2,1)S(1)} %collective-permute-done.16.theirs, f32[384,768]{1,0:T(8,128)S(1)} %get-tuple-element.35.across_part, f32[384,384]{1,0:T(8,128)S(1)} %get-tuple-element.36.rest_0_, ...), custom_call_target="tpu_custom_call" | custom-call | tf_op jit(solution)/shard_map/second_join/pallas_call | solution.py:353
  144.4 4.7 %collective-permute-start.21 = (bf16[384,768]{1,0:T(8,128)(2,1)S(1)}, bf16[384,768]{1,0:T(8,128)(2,1)S(1)}, u32[]{:S(2)}, u32[]{:S(2)}) collective-permute-start(bf16[384,768]{1,0:T(8,128)(2,1)S(1)} %get-tuple-element.38), channel_id=1, source_target_pairs={{0,1},{1,5},{2,0},{3,4},{4,3},{5,7},{6,2},{7,6},{8,9},{9,13},{10,8... | collective-permute-start | bytes 1769480 | tf_op jit(solution)/shard_map/ppermute | solution.py:493
  149.0 0.7 collective-permute-start.20
  149.8 19.4 %collective-permute-start.19 = (bf16[384,384]{1,0:T(8,128)(2,1)S(1)}, bf16[384,384]{1,0:T(8,128)(2,1)S(1)}, u32[]{:S(2)}, u32[]{:S(2)}) collective-permute-start(bf16[384,384]{1,0:T(8,128)(2,1)S(1)} %get-tuple-element.59), channel_id=1, source_target_pairs={{0,1},{2,3},{4,5},{6,7},{8,9},{10,11},{12,13},{14,15},{16,17},{18,... | collective-permute-start | bytes 884744 | tf_op jit(solution)/shard_map/ppermute | solution.py:506
  169.2 0.7 collective-permute-start.22
  169.9 2.6 %collective-permute-start.23 = (bf16[768,128]{1,0:T(8,128)(2,1)S(1)}, bf16[768,128]{1,0:T(8,128)(2,1)S(1)}, u32[]{:S(2)}, u32[]{:S(2)}) collective-permute-start(bf16[768,128]{1,0:T(8,128)(2,1)S(1)} %get-tuple-element.40), channel_id=1, source_target_pairs={{0,1},{1,5},{2,0},{3,4},{4,3},{5,7},{6,2},{7,6},{8,9},{9,13},{10,8... | collective-permute-start | bytes 589832 | tf_op jit(solution)/shard_map/ppermute | solution.py:493
  172.5 13.7 %collective-permute-done.23.other_corner = bf16[768,128]{1,0:T(8,128)(2,1)S(1)} collective-permute-done((bf16[768,128]{1,0:T(8,128)(2,1)S(1)}, bf16[768,128]{1,0:T(8,128)(2,1)S(1)}, u32[]{:S(2)}, u32[]{:S(2)}) %collective-permute-start.23) | collective-permute-done | bytes 196640 | tf_op jit(solution)/shard_map/ppermute | solution.py:493
  186.2 2.6 %assemble.1 = f32[384,1536]{1,0:T(8,128)} custom-call(f32[384,384]{1,0:T(8,128)S(1)} %get-tuple-element.60.link, bf16[384,384]{1,0:T(8,128)(2,1)S(1)} %collective-permute-done.19.passed, bf16[384,768]{1,0:T(8,128)(2,1)S(1)} %collective-permute-done.20.side, bf16[384,768]{1,0:T(8,128)(2,1)S(1)} %collective-permute-done.21.other_side, ...), custom_call_target="tpu_custom_call" | custom-call | tf_op jit(solution)/shard_map/assemble/pallas_call | solution.py:429
  (48 shorter events, 2.0 us)
Async XLA Ops:
  3.5 13.3 %collective-permute-start.8 = (s16[128,1152]{1,0:T(8,128)(2,1)S(1)}, s16[128,1152]{1,0:T(8,128)(2,1)S(1)}, u32[]{:S(2)}, u32[]{:S(2)}) collective-permute-start(s16[128,1152]{1,0:T(8,128)(2,1)S(1)} %fusion), channel_id=1, source_target_pairs={{0,16},{1,13},{2,18},{3,15},{4,20},{5,17},{6,22},{7,19},{8,24},{9,... | collective-permute-start | bytes 884744 | tf_op jit(solution)/shard_map/ppermute | solution.py:469
  6.5 30.3 %collective-permute-start.11 = (s16[128,1152]{1,0:T(8,128)(2,1)S(1)}, s16[128,1152]{1,0:T(8,128)(2,1)S(1)}, u32[]{:S(2)}, u32[]{:S(2)}) collective-permute-start(s16[128,1152]{1,0:T(8,128)(2,1)S(1)} %fusion), channel_id=1, source_target_pairs={{0,24},{1,21},{2,26},{3,23},{4,28},{5,25},{6,30},{7,27},{8,0},{9,2... | collective-permute-start | bytes 884744 | tf_op jit(solution)/shard_map/ppermute | solution.py:469
  8.0 26.9 %collective-permute-start.10 = (s16[128,1152]{1,0:T(8,128)(2,1)S(1)}, s16[128,1152]{1,0:T(8,128)(2,1)S(1)}, u32[]{:S(2)}, u32[]{:S(2)}) collective-permute-start(s16[128,1152]{1,0:T(8,128)(2,1)S(1)} %fusion), channel_id=1, source_target_pairs={{0,0},{1,29},{2,2},{3,31},{4,4},{5,1},{6,6},{7,3},{8,8},{9,5},{10,... | collective-permute-start | bytes 884744 | tf_op jit(solution)/shard_map/ppermute | solution.py:469
  8.6 24.9 %collective-permute-start.9 = (s16[128,1152]{1,0:T(8,128)(2,1)S(1)}, s16[128,1152]{1,0:T(8,128)(2,1)S(1)}, u32[]{:S(2)}, u32[]{:S(2)}) collective-permute-start(s16[128,1152]{1,0:T(8,128)(2,1)S(1)} %fusion), channel_id=1, source_target_pairs={{0,8},{1,5},{2,10},{3,7},{4,12},{5,9},{6,14},{7,11},{8,16},{9,13},... | collective-permute-start | bytes 884744 | tf_op jit(solution)/shard_map/ppermute | solution.py:469
  14.3 19.2 %copy-start.5 = (bf16[4112,128]{1,0:T(8,128)(2,1)S(1)}, bf16[4112,128]{1,0:T(8,128)(2,1)}, u32[]{:S(2)}) copy-start(bf16[4112,128]{1,0:T(8,128)(2,1)} %get-tuple-element.25) | copy-start | bytes 3158020
  14.3 62.9 %collective-permute-start = (bf16[4112,128]{1,0:T(8,128)(2,1)}, bf16[4112,128]{1,0:T(8,128)(2,1)S(1)}, u32[]{:S(2)}, u32[]{:S(2)}) collective-permute-start(bf16[4112,128]{1,0:T(8,128)(2,1)} %get-tuple-element.23), channel_id=1, source_target_pairs={{0,8},{1,12},{2,10},{3,14},{4,9},{5,13},{6,11},{7,15},{8,0},{9,4},... | collective-permute-start | bytes 3158024 | tf_op jit(solution)/shard_map/ppermute | solution.py:458
  16.8 60.4 %collective-permute-start.1 = (bf16[4112,128]{1,0:T(8,128)(2,1)}, bf16[4112,128]{1,0:T(8,128)(2,1)S(1)}, u32[]{:S(2)}, u32[]{:S(2)}) collective-permute-start(bf16[4112,128]{1,0:T(8,128)(2,1)} %get-tuple-element.24), channel_id=1, source_target_pairs={{0,16},{1,20},{2,18},{3,22},{4,17},{5,21},{6,19},{7,23},{8,24},{9,... | collective-permute-start | bytes 3158024 | tf_op jit(solution)/shard_map/ppermute | solution.py:458
  17.6 17.2 %copy-start.4 = (bf16[4112,128]{1,0:T(8,128)(2,1)S(1)}, bf16[4112,128]{1,0:T(8,128)(2,1)}, u32[]{:S(2)}) copy-start(bf16[4112,128]{1,0:T(8,128)(2,1)} %get-tuple-element.26) | copy-start | bytes 3158020
  33.5 54.0 %collective-permute-start.2 = (bf16[4112,128]{1,0:T(8,128)(2,1)S(1)}, bf16[4112,128]{1,0:T(8,128)(2,1)S(1)}, u32[]{:S(2)}, u32[]{:S(2)}) collective-permute-start(bf16[4112,128]{1,0:T(8,128)(2,1)S(1)} %copy-done.5), channel_id=1, source_target_pairs={{0,9},{1,13},{2,11},{3,15},{4,8},{5,12},{6,10},{7,14},{8,1},{9,5},... | collective-permute-start | bytes 3158024 | tf_op jit(solution)/shard_map/ppermute | solution.py:458
  34.9 55.6 %collective-permute-start.3 = (bf16[4112,128]{1,0:T(8,128)(2,1)S(1)}, bf16[4112,128]{1,0:T(8,128)(2,1)S(1)}, u32[]{:S(2)}, u32[]{:S(2)}) collective-permute-start(bf16[4112,128]{1,0:T(8,128)(2,1)S(1)} %copy-done.4), channel_id=1, source_target_pairs={{0,17},{1,21},{2,19},{3,23},{4,16},{5,20},{6,18},{7,22},{8,25},{9,... | collective-permute-start | bytes 3158024 | tf_op jit(solution)/shard_map/ppermute | solution.py:458
  36.8 1.6 collective-permute-start.15
  37.4 5.8 %copy-start.3 = (bf16[4112,128]{1,0:T(8,128)(2,1)S(1)}, bf16[4112,128]{1,0:T(8,128)(2,1)}, u32[]{:S(2)}) copy-start(bf16[4112,128]{1,0:T(8,128)(2,1)} %get-tuple-element.27) | copy-start | bytes 3158020
  38.5 1.6 collective-permute-start.14
  38.8 38.4 %copy-start.2 = (bf16[4112,128]{1,0:T(8,128)(2,1)S(1)}, bf16[4112,128]{1,0:T(8,128)(2,1)}, u32[]{:S(2)}) copy-start(bf16[4112,128]{1,0:T(8,128)(2,1)} %get-tuple-element.28) | copy-start | bytes 3158020
  40.1 1.6 collective-permute-start.13
  40.4 36.8 %copy-start.1 = (bf16[4112,128]{1,0:T(8,128)(2,1)S(1)}, bf16[4112,128]{1,0:T(8,128)(2,1)}, u32[]{:S(2)}) copy-start(bf16[4112,128]{1,0:T(8,128)(2,1)} %get-tuple-element.29) | copy-start | bytes 3158020
  40.5 47.0 %copy-start = (bf16[4112,128]{1,0:T(8,128)(2,1)S(1)}, bf16[4112,128]{1,0:T(8,128)(2,1)}, u32[]{:S(2)}) copy-start(bf16[4112,128]{1,0:T(8,128)(2,1)} %get-tuple-element.30) | copy-start | bytes 3158020
  41.6 1.6 collective-permute-start.12
  43.2 64.7 %collective-permute-start.4 = (bf16[4112,128]{1,0:T(8,128)(2,1)S(1)}, bf16[4112,128]{1,0:T(8,128)(2,1)S(1)}, u32[]{:S(2)}, u32[]{:S(2)}) collective-permute-start(bf16[4112,128]{1,0:T(8,128)(2,1)S(1)} %copy-done.3), channel_id=1, source_target_pairs={{0,24},{1,28},{2,26},{3,30},{4,25},{5,29},{6,27},{7,31},{8,16},{9,... | collective-permute-start | bytes 3158024 | tf_op jit(solution)/shard_map/ppermute | solution.py:458
  77.2 35.5 %collective-permute-start.5 = (bf16[4112,128]{1,0:T(8,128)(2,1)S(1)}, bf16[4112,128]{1,0:T(8,128)(2,1)S(1)}, u32[]{:S(2)}, u32[]{:S(2)}) collective-permute-start(bf16[4112,128]{1,0:T(8,128)(2,1)S(1)} %copy-done.2), channel_id=1, source_target_pairs={{0,25},{1,29},{2,27},{3,31},{4,24},{5,28},{6,26},{7,30},{8,17},{9,... | collective-permute-start | bytes 3158024 | tf_op jit(solution)/shard_map/ppermute | solution.py:458
  77.2 35.5 %collective-permute-start.6 = (bf16[4112,128]{1,0:T(8,128)(2,1)S(1)}, bf16[4112,128]{1,0:T(8,128)(2,1)S(1)}, u32[]{:S(2)}, u32[]{:S(2)}) collective-permute-start(bf16[4112,128]{1,0:T(8,128)(2,1)S(1)} %copy-done.1), channel_id=1, source_target_pairs={{0,0},{1,4},{2,2},{3,6},{4,1},{5,5},{6,3},{7,7},{8,8},{9,12},{10,1... | collective-permute-start | bytes 3158024 | tf_op jit(solution)/shard_map/ppermute | solution.py:458
  87.5 25.2 %collective-permute-start.7 = (bf16[4112,128]{1,0:T(8,128)(2,1)S(1)}, bf16[4112,128]{1,0:T(8,128)(2,1)S(1)}, u32[]{:S(2)}, u32[]{:S(2)}) collective-permute-start(bf16[4112,128]{1,0:T(8,128)(2,1)S(1)} %copy-done), channel_id=1, source_target_pairs={{0,1},{1,5},{2,3},{3,7},{4,0},{5,4},{6,2},{7,6},{8,9},{9,13},{10,1... | collective-permute-start | bytes 3158024 | tf_op jit(solution)/shard_map/ppermute | solution.py:458
  131.2 5.7 %collective-permute-start.16 = (bf16[1536,1024]{1,0:T(8,128)(2,1)S(1)}, bf16[1536,1024]{1,0:T(8,128)(2,1)S(1)}, u32[]{:S(2)}, u32[]{:S(2)}) collective-permute-start(bf16[1536,1024]{1,0:T(8,128)(2,1)S(1)} %couple.1.mine), channel_id=1, source_target_pairs={{0,4},{4,0},{8,12},{12,8},{16,20},{20,16},{24,28},{28,24},{1,5},{5... | collective-permute-start | bytes 9437192 | tf_op jit(solution)/shard_map/ppermute | solution.py:481
  139.2 10.5 %collective-permute-start.18 = (bf16[384,384]{1,0:T(8,128)(2,1)S(1)}, bf16[384,384]{1,0:T(8,128)(2,1)S(1)}, u32[]{:S(2)}, u32[]{:S(2)}) collective-permute-start(bf16[384,384]{1,0:T(8,128)(2,1)S(1)} %get-tuple-element.33), channel_id=1, source_target_pairs={{2,0},{3,4},{6,2},{7,6},{10,8},{11,12},{14,10},{15,14},{18,16},{19... | collective-permute-start | bytes 884744 | tf_op jit(solution)/shard_map/ppermute | solution.py:493
  140.5 9.2 %collective-permute-start.17 = (bf16[384,384]{1,0:T(8,128)(2,1)S(1)}, bf16[384,384]{1,0:T(8,128)(2,1)S(1)}, u32[]{:S(2)}, u32[]{:S(2)}) collective-permute-start(bf16[384,384]{1,0:T(8,128)(2,1)S(1)} %get-tuple-element.33), channel_id=1, source_target_pairs={{0,0},{1,4},{4,2},{5,6},{8,8},{9,12},{12,10},{13,14},{16,16},{17,2... | collective-permute-start | bytes 884744 | tf_op jit(solution)/shard_map/ppermute | solution.py:493
  144.4 41.8 %collective-permute-start.21 = (bf16[384,768]{1,0:T(8,128)(2,1)S(1)}, bf16[384,768]{1,0:T(8,128)(2,1)S(1)}, u32[]{:S(2)}, u32[]{:S(2)}) collective-permute-start(bf16[384,768]{1,0:T(8,128)(2,1)S(1)} %get-tuple-element.38), channel_id=1, source_target_pairs={{0,1},{1,5},{2,0},{3,4},{4,3},{5,7},{6,2},{7,6},{8,9},{9,13},{10,8... | collective-permute-start | bytes 1769480 | tf_op jit(solution)/shard_map/ppermute | solution.py:493
  149.0 37.2 %collective-permute-start.20 = (bf16[384,768]{1,0:T(8,128)(2,1)S(1)}, bf16[384,768]{1,0:T(8,128)(2,1)S(1)}, u32[]{:S(2)}, u32[]{:S(2)}) collective-permute-start(bf16[384,768]{1,0:T(8,128)(2,1)S(1)} %get-tuple-element.34), channel_id=1, source_target_pairs={{0,0},{1,4},{2,1},{3,5},{4,2},{5,6},{6,3},{7,7},{8,8},{9,12},{10,9... | collective-permute-start | bytes 1769480 | tf_op jit(solution)/shard_map/ppermute | solution.py:493
  149.8 36.4 %collective-permute-start.19 = (bf16[384,384]{1,0:T(8,128)(2,1)S(1)}, bf16[384,384]{1,0:T(8,128)(2,1)S(1)}, u32[]{:S(2)}, u32[]{:S(2)}) collective-permute-start(bf16[384,384]{1,0:T(8,128)(2,1)S(1)} %get-tuple-element.59), channel_id=1, source_target_pairs={{0,1},{2,3},{4,5},{6,7},{8,9},{10,11},{12,13},{14,15},{16,17},{18,... | collective-permute-start | bytes 884744 | tf_op jit(solution)/shard_map/ppermute | solution.py:506
  169.2 3.2 %collective-permute-start.22 = (bf16[768,128]{1,0:T(8,128)(2,1)S(1)}, bf16[768,128]{1,0:T(8,128)(2,1)S(1)}, u32[]{:S(2)}, u32[]{:S(2)}) collective-permute-start(bf16[768,128]{1,0:T(8,128)(2,1)S(1)} %get-tuple-element.39), channel_id=1, source_target_pairs={{0,0},{1,4},{2,1},{3,5},{4,2},{5,6},{6,3},{7,7},{8,8},{9,12},{10,9... | collective-permute-start | bytes 589832 | tf_op jit(solution)/shard_map/ppermute | solution.py:493
  169.9 16.3 %collective-permute-start.23 = (bf16[768,128]{1,0:T(8,128)(2,1)S(1)}, bf16[768,128]{1,0:T(8,128)(2,1)S(1)}, u32[]{:S(2)}, u32[]{:S(2)}) collective-permute-start(bf16[768,128]{1,0:T(8,128)(2,1)S(1)} %get-tuple-element.40), channel_id=1, source_target_pairs={{0,1},{1,5},{2,0},{3,4},{4,3},{5,7},{6,2},{7,6},{8,9},{9,13},{10,8... | collective-permute-start | bytes 589832 | tf_op jit(solution)/shard_map/ppermute | solution.py:493
where the time goes:
time: 189 us
  waiting for transfers between devices  102 us (54%)
  starting transfers between devices  46.2 us (24%)
  Pallas kernels  34.4 us (18%)
  other arithmetic  5.49 us (3%)
    ppermute x8, waiting for transfers between devices, per_device(): sent.append(lax.ppermute(message, AXES, pairs))  65.5 us
    ppermute x1, starting transfers between devices, per_device(): passed = lax.ppermute(link.astype(jnp.bfloat16), AXES, on)  19.4 us
    pallas_call x1, Pallas kernels, couple(): pl.pallas_call(functools.partial(couple_kernel, count, slots, edge), out_...  18.5 us
    ppermute x4, waiting for transfers between devices, per_device(): own.append(lax.ppermute(window, AXES, pairs))  15.9 us
    ppermute x6, waiting for transfers between devices, sent_to(): return lax.ppermute(array, AXES, pairs)  13.7 us
    ppermute x6, starting transfers between devices, sent_to(): return lax.ppermute(array, AXES, pairs)  10.7 us
    ppermute x8, starting transfers between devices, per_device(): sent.append(lax.ppermute(message, AXES, pairs))  8.75 us
    ppermute x4, starting transfers between devices, per_device(): own.append(lax.ppermute(window, AXES, pairs))  5.79 us
  transfers between devices with their start and end apart: 24, of which 12 were waited for; matrix products, arithmetic and copies ran while one was open for 1% of the time, Pallas kernels for 6%

commit v1 on v0

--- a/solution.py
+++ b/solution.py
@@ -136,8 +136,7 @@
 def couple_kernel(count, slots, edge, *rest):
     messages, rest = rest[:count], rest[count:]
     coarse, fine, rest = rest[:STOPS], rest[STOPS : 2 * STOPS], rest[2 * STOPS :]
-    result, held, basis, basis_rest, dense, made, rest = *rest[:6], rest[6:]
-    label_blocks, label_rows, labels, tile_sem, basis_sem, label_sem, out_sem = rest
+    result, basis, basis_rest, dense, made, label_rows, labels, basis_sem, out_sem = rest
     core = lax.axis_index("blk") % 2
     loads = []
     for at in range(STOPS // 2):
@@ -146,43 +145,38 @@
             for ref, target in ((coarse[half + at], basis), (fine[half + at], basis_rest)):
                 loads.append(pltpu.make_async_copy(ref, target.at[rows], basis_sem.at[len(loads)]))
     height = slots * edge
-    label_loads = [
-        pltpu.make_async_copy(ref.at[pl.ds(height, LABEL_ROWS)], label_blocks.at[at], label_sem.at[at])
-        for at, ref in enumerate(messages)
-    ]
-    copies = [
-        pltpu.make_async_copy(ref.at[pl.ds(0, height)], held.at[at], tile_sem.at[at]) for at, ref in enumerate(messages)
-    ]
-    for copy in label_loads + copies + loads:
-        copy.start()
-    dense[...] = jnp.zeros_like(dense)
-    for at, copy in enumerate(label_loads):
-        copy.wait()
-        label_rows[pl.ds(at, 1), :] = label_blocks[at].astype(jnp.float32)[:1].astype(jnp.int32)
+    for load in loads:
+        load.start()
+    for at, message in enumerate(messages):
+        row = message[pl.ds(height, LABEL_ROWS), :].astype(jnp.float32)[:1]
+        filled = jnp.sum((row >= 0.0).astype(jnp.float32), axis=1, keepdims=True)
+        lane = lax.broadcasted_iota(jnp.int32, row.shape, 1)
+        label_rows[pl.ds(at, 1), :] = jnp.where(lane == edge - 1, filled, row).astype(jnp.int32)
     copy = pltpu.make_async_copy(label_rows, labels, out_sem)
     copy.start()
+    dense[...] = jnp.zeros_like(dense)
     copy.wait()
-    for at, copy in enumerate(copies):
-        copy.wait()
-
-        @pl.loop(0, slots)
-        def _(slot):
-            label = labels[at, slot]
-
-            @pl.when(label >= 0)
-            def _():
-                rows = pl.ds(pl.multiple_of(label // STOPS * edge, edge), edge)
-                columns = pl.ds(pl.multiple_of(label % STOPS * edge, edge), edge)
-                tile = held[at, pl.ds(pl.multiple_of(slot * edge, edge), edge), :]
-                dense[rows, columns] += tile.astype(jnp.float32)
+    together = min(4, slots)
+    for at, message in enumerate(messages):
+
+        @pl.loop(0, (labels[at, edge - 1] + together - 1) // together)
+        def _(group):
+            for inner in range(together):
+                slot = group * together + inner
+                label = labels[at, slot]
+
+                @pl.when(label >= 0)
+                def _():
+                    rows = pl.ds(pl.multiple_of(label // STOPS * edge, edge), edge)
+                    columns = pl.ds(pl.multiple_of(label % STOPS * edge, edge), edge)
+                    tile = message[pl.ds(pl.multiple_of(slot * edge, edge), edge), :]
+                    dense[rows, columns] += tile.astype(jnp.float32)
 
     for load in loads:
         load.wait()
     step = PANEL // 4
-
-    @pl.loop(0, 4)
-    def _(at):
-        rows = pl.ds(pl.multiple_of(at * step, step), step)
+    for start in range(0, PANEL, step):
+        rows = slice(start, start + step)
         value = dense[rows, :]
         high = value.astype(jnp.bfloat16)
         low = (value - high.astype(jnp.float32)).astype(jnp.bfloat16)
@@ -191,7 +185,6 @@
         sums += jnp.dot(high, basis[...], preferred_element_type=jnp.float32)
         made[rows, :] = sums.astype(jnp.bfloat16)
         pltpu.make_async_copy(made.at[rows], result.at[rows], out_sem).start()
-
     pltpu.make_async_copy(made, result, out_sem).wait()
 
 
@@ -200,20 +193,17 @@
     return pl.pallas_call(
         functools.partial(couple_kernel, count, slots, edge),
         out_shape=jax.ShapeDtypeStruct((PANEL, NOCC), jnp.bfloat16),
-        in_specs=[pl.BlockSpec(memory_space=pl.ANY)] * len(operands),
+        in_specs=[pl.BlockSpec(memory_space=pltpu.VMEM)] * count
+        + [pl.BlockSpec(memory_space=pl.ANY)] * (2 * STOPS),
         out_specs=pl.BlockSpec(memory_space=pl.ANY),
         scratch_shapes=[
-            pltpu.VMEM((count, slots * edge, edge), jnp.bfloat16),
             pltpu.VMEM((STOPS * edge, NOCC), jnp.bfloat16),
             pltpu.VMEM((STOPS * edge, NOCC), jnp.bfloat16),
             pltpu.VMEM((PANEL, STOPS * edge), jnp.float32),
             pltpu.VMEM((PANEL, NOCC), jnp.bfloat16),
-            pltpu.VMEM((count, LABEL_ROWS, edge), jnp.bfloat16),
             pltpu.VMEM((count, edge), jnp.int32),
             pltpu.SMEM((count, edge), jnp.int32),
-            pltpu.SemaphoreType.DMA((count,)),
             pltpu.SemaphoreType.DMA((2 * STOPS,)),
-            pltpu.SemaphoreType.DMA((count,)),
             pltpu.SemaphoreType.DMA,
         ],
         compiler_params=pltpu.CompilerParams(vmem_limit_bytes=36 * 1024 * 1024),
@@ -224,12 +214,30 @@
 STEPS = 32000.0
 
 
-def coded(value):
+def window_kernel(start, green, result, held, sem):
+    wide = held.shape[1]
+    first = jnp.minimum(start[0] // 128 * 128, green.shape[1] - wide)
+    copy = pltpu.make_async_copy(green.at[:, pl.ds(pl.multiple_of(first, 128), wide)], held, sem)
+    copy.start()
+    copy.wait()
+    value = pltpu.roll(held[...], (wide + first - start[0]) % wide, 1)[:, :NOCC]
     top = jnp.max(jnp.abs(value), axis=1, keepdims=True)
     scale_code = jnp.ceil(jnp.log2(jnp.maximum(top, 1e-30)) * 256.0)
-    steps = jnp.round(value * (STEPS / jnp.exp2(scale_code / 256.0)))
-    whole = jnp.concatenate([steps, jnp.broadcast_to(scale_code, (value.shape[0], 128))], axis=1)
-    return whole.astype(jnp.int32).astype(jnp.int16)
+    steps = jnp.round(value * (STEPS / jnp.exp2(scale_code * (1.0 / 256.0))))
+    result[:, :NOCC] = steps.astype(jnp.int32).astype(jnp.int16)
+    result[:, NOCC:] = jnp.broadcast_to(scale_code, (value.shape[0], 128)).astype(jnp.int32).astype(jnp.int16)
+
+
+def coded_window(green, start):
+    rows = green.shape[0]
+    return pl.pallas_call(
+        window_kernel,
+        out_shape=jax.ShapeDtypeStruct((rows, NOCC + 128), jnp.int16),
+        in_specs=[pl.BlockSpec(memory_space=pltpu.SMEM), pl.BlockSpec(memory_space=pl.ANY)],
+        out_specs=pl.BlockSpec(memory_space=pltpu.VMEM),
+        scratch_shapes=[pltpu.VMEM((rows, NOCC + 128), jnp.float32), pltpu.SemaphoreType.DMA],
+        name="window",
+    )(start, green)
 
 
 def decoded(code, width):
@@ -372,32 +380,21 @@
     )(theirs, across_part, corner_part, other_corner_part)
 
 
-def assemble_kernel(piece, edge, factor, link, passed, side, other_side, corner, other_corner, result, *rest):
-    made, rest = rest[0], rest[1:]
-    held, sems, out_sem = rest[:6], rest[6], rest[7]
+def near_kernel(piece, edge, factor, link, passed, corner, other_corner, result, made, *rest):
+    held, sems, out_sem = rest[:4], rest[4], rest[5]
     half = 2 * piece
     virt = lax.axis_index("virt")
-    order = (side, other_side, corner, other_corner, link, passed)
-    copies = [pltpu.make_async_copy(ref, target, sems.at[at]) for at, (ref, target) in enumerate(zip(order, held))]
+    operands = (corner, other_corner, link, passed)
+    copies = [pltpu.make_async_copy(ref, target, sems.at[at]) for at, (ref, target) in enumerate(zip(operands, held))]
     for copy in copies:
         copy.start()
-    side_h, other_side_h, corner_h, other_corner_h, link_h, passed_h = held
+    corner_h, other_corner_h, link_h, passed_h = held
 
     def store(start, value):
-        made[:, pl.ds(pl.multiple_of(start, edge), value.shape[1])] = value * factor
-
-    def put(start):
-        columns = pl.ds(pl.multiple_of(start, edge), half)
-        copy = pltpu.make_async_copy(made.at[:, columns], result.at[:, columns], out_sem)
-        copy.start()
-
-    near, far = virt // 2 * half, (1 - virt // 2) * half
+        made[:, pl.ds(pl.multiple_of(start, edge), piece)] = value * factor
+
     copies[0].wait()
     copies[1].wait()
-    store(far, side_h[...].astype(jnp.float32) + other_side_h[...].astype(jnp.float32))
-    put(far)
-    copies[2].wait()
-    copies[3].wait()
     count = piece // edge
     blocks = {}
     for at, place in enumerate(upper_blocks(count)):
@@ -407,36 +404,68 @@
         jnp.concatenate([blocks[i, j] if i <= j else blocks[j, i].T for j in range(count)], axis=1)
         for i in range(count)
     ]
-    store(near + virt % 2 * piece, jnp.concatenate(rows, axis=0))
-    copies[4].wait()
-    copies[5].wait()
+    store(virt % 2 * piece, jnp.concatenate(rows, axis=0))
+    copies[2].wait()
+    copies[3].wait()
 
     @pl.when(virt % 2 == 0)
     def _():
-        store(near + piece, link_h[...])
+        store(piece, link_h[...])
 
     @pl.when(virt % 2 == 1)
     def _():
-        store(near, passed_h[...].astype(jnp.float32).T)
-
-    put(near)
-    pltpu.make_async_copy(made, result, out_sem).wait()
+        store(0, passed_h[...].astype(jnp.float32).T)
+
+    columns = pl.ds(pl.multiple_of(virt // 2 * half, half), half)
+    copy = pltpu.make_async_copy(made, result.at[:, columns], out_sem)
+    copy.start()
+    copy.wait()
+
+
+def far_kernel(factor, begun, side, other_side, result, made, side_h, other_side_h, sems):
+    half = made.shape[1]
+    copies = [
+        pltpu.make_async_copy(ref, target, sems.at[at])
+        for at, (ref, target) in enumerate(((side, side_h), (other_side, other_side_h)))
+    ]
+    for copy in copies:
+        copy.start()
+    for copy in copies:
+        copy.wait()
+    made[...] = (side_h[...].astype(jnp.float32) + other_side_h[...].astype(jnp.float32)) * factor
+    columns = pl.ds(pl.multiple_of((1 - lax.axis_index("virt") // 2) * half, half), half)
+    copy = pltpu.make_async_copy(made, result.at[:, columns], sems.at[2])
+    copy.start()
+    copy.wait()
 
 
 def assemble(link, passed, sides, corners, piece, edge, factor):
-    operands = (link, passed, *sides, *corners)
-    width = 4 * piece
-    return pl.pallas_call(
-        functools.partial(assemble_kernel, piece, edge, factor),
-        out_shape=jax.ShapeDtypeStruct((piece, width), jnp.float32),
-        in_specs=[pl.BlockSpec(memory_space=pl.ANY)] * len(operands),
-        out_specs=pl.BlockSpec(memory_space=pl.ANY),
-        scratch_shapes=[pltpu.VMEM((piece, width), jnp.float32)]
-        + [pltpu.VMEM(array.shape, array.dtype) for array in (*sides, *corners, link, passed)]
-        + [pltpu.SemaphoreType.DMA((6,)), pltpu.SemaphoreType.DMA],
+    half = 2 * piece
+    result = jax.ShapeDtypeStruct((piece, 2 * half), jnp.float32)
+    anywhere = pl.BlockSpec(memory_space=pl.ANY)
+    begun = pl.pallas_call(
+        functools.partial(near_kernel, piece, edge, factor),
+        out_shape=result,
+        in_specs=[anywhere] * 4,
+        out_specs=anywhere,
+        scratch_shapes=[pltpu.VMEM((piece, half), jnp.float32)]
+        + [pltpu.VMEM(array.shape, array.dtype) for array in (*corners, link, passed)]
+        + [pltpu.SemaphoreType.DMA((4,)), pltpu.SemaphoreType.DMA],
         compiler_params=pltpu.CompilerParams(vmem_limit_bytes=20 * 1024 * 1024),
-        name="assemble",
-    )(*operands)
+        name="near_half",
+    )(link, passed, *corners)
+    return pl.pallas_call(
+        functools.partial(far_kernel, factor),
+        out_shape=result,
+        in_specs=[anywhere] * 3,
+        out_specs=anywhere,
+        input_output_aliases={0: 0},
+        scratch_shapes=[pltpu.VMEM((piece, half), jnp.float32)]
+        + [pltpu.VMEM(array.shape, array.dtype) for array in sides]
+        + [pltpu.SemaphoreType.DMA((3,))],
+        compiler_params=pltpu.CompilerParams(vmem_limit_bytes=20 * 1024 * 1024),
+        name="far_half",
+    )(begun, *sides)
 
 
 def per_device(integral_tiles, tile_panel, tile_row, tile_col, green_factor, window_start):
@@ -457,7 +486,7 @@
         ]
         sent.append(lax.ppermute(message, AXES, pairs))
 
-    window = coded(lax.dynamic_slice_in_dim(green_factor, window_start[0], NOCC, 1))
+    window = coded_window(green_factor, window_start)
     own = []
     for at in range(middle):
         pairs = []

time: 189 us -> 187 us (0.989)
  other arithmetic: 5.49 us -> 2.76 us
    pallas_call x1, Pallas kernels: 18.5 us -> 15.4 us  [couple(): pl.pallas_call(functools.partial(couple_kernel, count, slots, edge), out_...]
    pallas_call x1 -> x3, Pallas kernels: 2.56 us -> 5.51 us  [the longest x1 2.15 us: coded_window(): pl.pallas_call(window_kernel, out_shape=jax.ShapeDtypeStruct((rows, NOCC...]
    ppermute x1, starting transfers between devices: 19.4 us -> 17.2 us  [per_device(): passed = lax.ppermute(link.astype(jnp.bfloat16), AXES, on)]
  transfers between devices with their start and end apart: 24 -> 24, of which waited for: 12 -> 12; matrix products, arithmetic and copies ran while one was open for 1% -> 1% of each run, Pallas kernels for 6% -> 7%
where the time goes in v1:
time: 187 us
  waiting for transfers between devices  103 us (55%)
  starting transfers between devices  45.8 us (24%)
  Pallas kernels  34.3 us (18%)
  other arithmetic  2.76 us (1%)
    ppermute x8, waiting for transfers between devices, per_device(): sent.append(lax.ppermute(message, AXES, pairs))  65.2 us
    ppermute x1, starting transfers between devices, per_device(): passed = lax.ppermute(link.astype(jnp.bfloat16), AXES, on)  17.2 us
    ppermute x4, waiting for transfers between devices, per_device(): own.append(lax.ppermute(window, AXES, pairs))  15.4 us
    pallas_call x1, Pallas kernels, couple(): pl.pallas_call(functools.partial(couple_kernel, count, slots, edge), out_...  15.4 us
    ppermute x6, waiting for transfers between devices, sent_to(): return lax.ppermute(array, AXES, pairs)  15.3 us
    ppermute x6, starting transfers between devices, sent_to(): return lax.ppermute(array, AXES, pairs)  11.9 us
    ppermute x8, starting transfers between devices, per_device(): sent.append(lax.ppermute(message, AXES, pairs))  9.09 us
    ppermute x4, starting transfers between devices, per_device(): own.append(lax.ppermute(window, AXES, pairs))  6.68 us
  transfers between devices with their start and end apart: 24, of which 12 were waited for; matrix products, arithmetic and copies ran while one was open for 1% of the time, Pallas kernels for 7%

profile of v1, /device:TPU:0, one launch (start us, length us, event | category | flops | bytes accessed | tf_op | source)
XLA Modules:
  0.0 187.1 jit_solution(10914763682206480072)
XLA Ops:
  0.7 2.2 %window.1 = s16[128,1152]{1,0:T(8,128)(2,1)} custom-call(s32[1]{0:T(128)S(6)} %copy.9.start, f32[128,8192]{1,0:T(8,128)} %green.1), custom_call_target="tpu_custom_call" | custom-call | tf_op jit(solution)/shard_map/window/pallas_call | solution.py:233
  2.8 3.0 %collective-permute-start.8 = (s16[128,1152]{1,0:T(8,128)(2,1)}, s16[128,1152]{1,0:T(8,128)(2,1)S(1)}, u32[]{:S(2)}, u32[]{:S(2)}) collective-permute-start(s16[128,1152]{1,0:T(8,128)(2,1)} %window.1), channel_id=1, source_target_pairs={{0,16},{1,13},{2,18},{3,15},{4,20},{5,17},{6,22},{7,19},{8,24},{9,... | collective-permute-start | bytes 884744 | tf_op jit(solution)/shard_map/ppermute | solution.py:498
  5.9 1.4 collective-permute-start.11
  7.3 1.6 collective-permute-start.10
  8.9 0.6 collective-permute-start.9
  9.5 5.0 %pack.1 = (bf16[4112,128]{1,0:T(8,128)(2,1)}, bf16[4112,128]{1,0:T(8,128)(2,1)}, bf16[4112,128]{1,0:T(8,128)(2,1)}, bf16[4112,128]{1,0:T(8,128)(2,1)}, bf16[4112...) custom-call(s32[128]{0:T(128)} %bitcast.4, ...), custom_call_target="tpu_custom_call" | custom-call | tf_op jit(solution)/shard_map/pack/pallas_call | solution.py:111
  14.5 2.5 %collective-permute-start = (bf16[4112,128]{1,0:T(8,128)(2,1)}, bf16[4112,128]{1,0:T(8,128)(2,1)S(1)}, u32[]{:S(2)}, u32[]{:S(2)}) collective-permute-start(bf16[4112,128]{1,0:T(8,128)(2,1)} %get-tuple-element.23), channel_id=1, source_target_pairs={{0,8},{1,12},{2,10},{3,14},{4,9},{5,13},{6,11},{7,15},{8,0},{9,4},... | collective-permute-start | bytes 3158024 | tf_op jit(solution)/shard_map/ppermute | solution.py:487
  17.0 0.5 collective-permute-start.1
  17.7 0.2 fusion
  17.9 15.4 %collective-permute-done.9 = s16[128,1152]{1,0:T(8,128)(2,1)S(1)} collective-permute-done((s16[128,1152]{1,0:T(8,128)(2,1)}, s16[128,1152]{1,0:T(8,128)(2,1)S(1)}, u32[]{:S(2)}, u32[]{:S(2)}) %collective-permute-start.9) | collective-permute-done | bytes 294944 | tf_op jit(solution)/shard_map/ppermute | solution.py:498
  33.3 0.7 collective-permute-start.2
  34.2 0.2 fusion.1
  34.4 1.7 collective-permute-start.3
  36.3 0.2 fusion.2
  36.4 0.3 collective-permute-start.15
  36.9 0.1 fusion.3
  37.1 1.0 collective-permute-done.15
  38.1 0.2 collective-permute-start.14
  38.4 1.3 collective-permute-done.14
  39.7 0.2 collective-permute-start.13
  40.0 1.3 collective-permute-done.13
  41.2 0.2 collective-permute-start.12
  41.9 0.9 collective-permute-done.12
  42.8 2.5 %collective-permute-start.4 = (bf16[4112,128]{1,0:T(8,128)(2,1)S(1)}, bf16[4112,128]{1,0:T(8,128)(2,1)S(1)}, u32[]{:S(2)}, u32[]{:S(2)}) collective-permute-start(bf16[4112,128]{1,0:T(8,128)(2,1)S(1)} %copy-done.3), channel_id=1, source_target_pairs={{0,24},{1,28},{2,26},{3,30},{4,25},{5,29},{6,27},{7,31},{8,16},{9,... | collective-permute-start | bytes 3158024 | tf_op jit(solution)/shard_map/ppermute | solution.py:487
  45.4 30.8 %collective-permute-done.rest_0_ = bf16[4112,128]{1,0:T(8,128)(2,1)S(1)} collective-permute-done((bf16[4112,128]{1,0:T(8,128)(2,1)}, bf16[4112,128]{1,0:T(8,128)(2,1)S(1)}, u32[]{:S(2)}, u32[]{:S(2)}) %collective-permute-start) | collective-permute-done | bytes 1052704 | tf_op jit(solution)/shard_map/ppermute | solution.py:487
  76.3 0.7 collective-permute-start.6
  77.0 9.9 %collective-permute-done.2.rest_2_ = bf16[4112,128]{1,0:T(8,128)(2,1)S(1)} collective-permute-done((bf16[4112,128]{1,0:T(8,128)(2,1)S(1)}, bf16[4112,128]{1,0:T(8,128)(2,1)S(1)}, u32[]{:S(2)}, u32[]{:S(2)}) %collective-permute-start.2) | collective-permute-done | bytes 1052704 | tf_op jit(solution)/shard_map/ppermute | solution.py:487
  86.9 0.5 collective-permute-start.7
  87.5 0.1 fusion.7
  88.0 0.1 fusion.4
  88.1 3.5 %collective-permute-done.3.rest_3_ = bf16[4112,128]{1,0:T(8,128)(2,1)S(1)} collective-permute-done((bf16[4112,128]{1,0:T(8,128)(2,1)S(1)}, bf16[4112,128]{1,0:T(8,128)(2,1)S(1)}, u32[]{:S(2)}, u32[]{:S(2)}) %collective-permute-start.3) | collective-permute-done | bytes 1052704 | tf_op jit(solution)/shard_map/ppermute | solution.py:487
  91.7 16.3 %collective-permute-done.4.rest_4_ = bf16[4112,128]{1,0:T(8,128)(2,1)S(1)} collective-permute-done((bf16[4112,128]{1,0:T(8,128)(2,1)S(1)}, bf16[4112,128]{1,0:T(8,128)(2,1)S(1)}, u32[]{:S(2)}, u32[]{:S(2)}) %collective-permute-start.4) | collective-permute-done | bytes 1052704 | tf_op jit(solution)/shard_map/ppermute | solution.py:487
  108.0 4.6 %collective-permute-done.5.rest_5_ = bf16[4112,128]{1,0:T(8,128)(2,1)S(1)} collective-permute-done((bf16[4112,128]{1,0:T(8,128)(2,1)S(1)}, bf16[4112,128]{1,0:T(8,128)(2,1)S(1)}, u32[]{:S(2)}, u32[]{:S(2)}) %collective-permute-start.5) | collective-permute-done | bytes 1052704 | tf_op jit(solution)/shard_map/ppermute | solution.py:487
  112.6 15.4 %couple.1.mine = bf16[1536,1024]{1,0:T(8,128)(2,1)S(1)} custom-call(bf16[4112,128]{1,0:T(8,128)(2,1)S(1)} %collective-permute-done.rest_0_, bf16[4112,128]{1,0:T(8,128)(2,1)S(1)} %collective-permute-done.1.rest_1_, bf16[4112,128]{1,0:T(8,128)(2,1)S(1)} %collective-permute-done.2.rest_2_, bf16[4112,128]{1,0:T(8,128)(2,1)S(1)} %collective-permute-done.3.rest_3_, ...), custom_call_target="tpu_custom_call" | custom-call | tf_op jit(solution)/shard_map/couple/pallas_call | solution.py:193
  128.1 3.1 %own_join.1 = (f32[384,384]{1,0:T(8,128)S(1)}, f32[384,768]{1,0:T(8,128)S(1)}, f32[384,768]{1,0:T(8,128)S(1)}, f32[384,384]{1,0:T(8,128)S(1)}, f32[384,384]{1,0:T(8,128)S(1)}) custom-call(bf16[1536,1024]{1,0:T(8,128)(2,1)S(1)} %couple.1.mine), custom_call_target="tpu_custom_call" | custom-call | tf_op jit(solution)/shard_map/own_join/pallas_call | solution.py:288
  131.2 2.5 %collective-permute-done.16.theirs = bf16[1536,1024]{1,0:T(8,128)(2,1)S(1)} collective-permute-done((bf16[1536,1024]{1,0:T(8,128)(2,1)S(1)}, bf16[1536,1024]{1,0:T(8,128)(2,1)S(1)}, u32[]{:S(2)}, u32[]{:S(2)}) %collective-permute-start.16) | collective-permute-done | bytes 3145760 | tf_op jit(solution)/shard_map/ppermute | solution.py:510
  133.7 2.2 %first_join.1 = (bf16[384,384]{1,0:T(8,128)(2,1)S(1)}, bf16[384,768]{1,0:T(8,128)(2,1)S(1)}) custom-call(bf16[1536,1024]{1,0:T(8,128)(2,1)S(1)} %collective-permute-done.16.theirs, f32[384,384]{1,0:T(8,128)S(1)} %get-tuple-element.31.between_part, f32[384,768]{1,0:T(8,128)S(1)} %get-tuple-element.32.across_part), custom_call_target="tpu_custom_call" | custom-call | tf_op jit(solution)/shard_map/first_join/pallas_call | solution.py:338
  136.0 1.3 collective-permute-start.18
  137.3 0.7 collective-permute-start.17
  137.9 3.0 %second_join.1 = (bf16[384,768]{1,0:T(8,128)(2,1)S(1)}, bf16[768,128]{1,0:T(8,128)(2,1)S(1)}, bf16[768,128]{1,0:T(8,128)(2,1)S(1)}) custom-call(bf16[1536,1024]{1,0:T(8,128)(2,1)S(1)} %collective-permute-done.16.theirs, f32[384,768]{1,0:T(8,128)S(1)} %get-tuple-element.34.across_part, f32[384,384]{1,0:T(8,128)S(1)} %get-tuple-element.35.rest_0_, ...), custom_call_target="tpu_custom_call" | custom-call | tf_op jit(solution)/shard_map/second_join/pallas_call | solution.py:361
  141.0 5.8 %collective-permute-start.23 = (bf16[384,768]{1,0:T(8,128)(2,1)S(1)}, bf16[384,768]{1,0:T(8,128)(2,1)S(1)}, u32[]{:S(2)}, u32[]{:S(2)}) collective-permute-start(bf16[384,768]{1,0:T(8,128)(2,1)S(1)} %get-tuple-element.40), channel_id=1, source_target_pairs={{0,1},{1,5},{2,0},{3,4},{4,3},{5,7},{6,2},{7,6},{8,9},{9,13},{10,8... | collective-permute-start | bytes 1769480 | tf_op jit(solution)/shard_map/ppermute | solution.py:522
  146.8 0.7 collective-permute-start.22
  147.6 17.2 %collective-permute-start.19 = (bf16[384,384]{1,0:T(8,128)(2,1)S(1)}, bf16[384,384]{1,0:T(8,128)(2,1)S(1)}, u32[]{:S(2)}, u32[]{:S(2)}) collective-permute-start(bf16[384,384]{1,0:T(8,128)(2,1)S(1)} %get-tuple-element.57), channel_id=1, source_target_pairs={{0,1},{2,3},{4,5},{6,7},{8,9},{10,11},{12,13},{14,15},{16,17},{18,... | collective-permute-start | bytes 884744 | tf_op jit(solution)/shard_map/ppermute | solution.py:535
  164.8 0.7 collective-permute-start.20
  165.5 2.7 %collective-permute-start.21 = (bf16[768,128]{1,0:T(8,128)(2,1)S(1)}, bf16[768,128]{1,0:T(8,128)(2,1)S(1)}, u32[]{:S(2)}, u32[]{:S(2)}) collective-permute-start(bf16[768,128]{1,0:T(8,128)(2,1)S(1)} %get-tuple-element.38), channel_id=1, source_target_pairs={{0,1},{1,5},{2,0},{3,4},{4,3},{5,7},{6,2},{7,6},{8,9},{9,13},{10,8... | collective-permute-start | bytes 589832 | tf_op jit(solution)/shard_map/ppermute | solution.py:522
  168.2 15.3 %collective-permute-done.21.other_corner = bf16[768,128]{1,0:T(8,128)(2,1)S(1)} collective-permute-done((bf16[768,128]{1,0:T(8,128)(2,1)S(1)}, bf16[768,128]{1,0:T(8,128)(2,1)S(1)}, u32[]{:S(2)}, u32[]{:S(2)}) %collective-permute-start.21) | collective-permute-done | bytes 196640 | tf_op jit(solution)/shard_map/ppermute | solution.py:522
  183.5 1.9 %near_half.1.begun = f32[384,1536]{1,0:T(8,128)} custom-call(f32[384,384]{1,0:T(8,128)S(1)} %get-tuple-element.58.link, bf16[384,384]{1,0:T(8,128)(2,1)S(1)} %collective-permute-done.19.passed, bf16[768,128]{1,0:T(8,128)(2,1)S(1)} %collective-permute-done.20.corner, bf16[768,128]{1,0:T(8,128)(2,1)S(1)} %collective-permute-done.21.other_corner), custom_call_target="tpu_custom_call" | custom-call | tf_op jit(solution)/shard_map/near_half/pallas_call | solution.py:446
  185.5 1.4 far_half.1
  (45 shorter events, 2.0 us)
Async XLA Ops:
  2.8 14.2 %collective-permute-start.8 = (s16[128,1152]{1,0:T(8,128)(2,1)}, s16[128,1152]{1,0:T(8,128)(2,1)S(1)}, u32[]{:S(2)}, u32[]{:S(2)}) collective-permute-start(s16[128,1152]{1,0:T(8,128)(2,1)} %window.1), channel_id=1, source_target_pairs={{0,16},{1,13},{2,18},{3,15},{4,20},{5,17},{6,22},{7,19},{8,24},{9,... | collective-permute-start | bytes 884744 | tf_op jit(solution)/shard_map/ppermute | solution.py:498
  5.9 30.6 %collective-permute-start.11 = (s16[128,1152]{1,0:T(8,128)(2,1)}, s16[128,1152]{1,0:T(8,128)(2,1)S(1)}, u32[]{:S(2)}, u32[]{:S(2)}) collective-permute-start(s16[128,1152]{1,0:T(8,128)(2,1)} %window.1), channel_id=1, source_target_pairs={{0,24},{1,21},{2,26},{3,23},{4,28},{5,25},{6,30},{7,27},{8,0},{9,2... | collective-permute-start | bytes 884744 | tf_op jit(solution)/shard_map/ppermute | solution.py:498
  7.3 27.1 %collective-permute-start.10 = (s16[128,1152]{1,0:T(8,128)(2,1)}, s16[128,1152]{1,0:T(8,128)(2,1)S(1)}, u32[]{:S(2)}, u32[]{:S(2)}) collective-permute-start(s16[128,1152]{1,0:T(8,128)(2,1)} %window.1), channel_id=1, source_target_pairs={{0,0},{1,29},{2,2},{3,31},{4,4},{5,1},{6,6},{7,3},{8,8},{9,5},{10,... | collective-permute-start | bytes 884744 | tf_op jit(solution)/shard_map/ppermute | solution.py:498
  8.9 24.4 %collective-permute-start.9 = (s16[128,1152]{1,0:T(8,128)(2,1)}, s16[128,1152]{1,0:T(8,128)(2,1)S(1)}, u32[]{:S(2)}, u32[]{:S(2)}) collective-permute-start(s16[128,1152]{1,0:T(8,128)(2,1)} %window.1), channel_id=1, source_target_pairs={{0,8},{1,5},{2,10},{3,7},{4,12},{5,9},{6,14},{7,11},{8,16},{9,13},... | collective-permute-start | bytes 884744 | tf_op jit(solution)/shard_map/ppermute | solution.py:498
  14.5 18.8 %copy-start.5 = (bf16[4112,128]{1,0:T(8,128)(2,1)S(1)}, bf16[4112,128]{1,0:T(8,128)(2,1)}, u32[]{:S(2)}) copy-start(bf16[4112,128]{1,0:T(8,128)(2,1)} %get-tuple-element.25) | copy-start | bytes 3158020
  14.5 61.7 %collective-permute-start = (bf16[4112,128]{1,0:T(8,128)(2,1)}, bf16[4112,128]{1,0:T(8,128)(2,1)S(1)}, u32[]{:S(2)}, u32[]{:S(2)}) collective-permute-start(bf16[4112,128]{1,0:T(8,128)(2,1)} %get-tuple-element.23), channel_id=1, source_target_pairs={{0,8},{1,12},{2,10},{3,14},{4,9},{5,13},{6,11},{7,15},{8,0},{9,4},... | collective-permute-start | bytes 3158024 | tf_op jit(solution)/shard_map/ppermute | solution.py:487
  17.0 59.3 %collective-permute-start.1 = (bf16[4112,128]{1,0:T(8,128)(2,1)}, bf16[4112,128]{1,0:T(8,128)(2,1)S(1)}, u32[]{:S(2)}, u32[]{:S(2)}) collective-permute-start(bf16[4112,128]{1,0:T(8,128)(2,1)} %get-tuple-element.24), channel_id=1, source_target_pairs={{0,16},{1,20},{2,18},{3,22},{4,17},{5,21},{6,19},{7,23},{8,24},{9,... | collective-permute-start | bytes 3158024 | tf_op jit(solution)/shard_map/ppermute | solution.py:487
  17.9 16.5 %copy-start.4 = (bf16[4112,128]{1,0:T(8,128)(2,1)S(1)}, bf16[4112,128]{1,0:T(8,128)(2,1)}, u32[]{:S(2)}) copy-start(bf16[4112,128]{1,0:T(8,128)(2,1)} %get-tuple-element.26) | copy-start | bytes 3158020
  33.3 53.6 %collective-permute-start.2 = (bf16[4112,128]{1,0:T(8,128)(2,1)S(1)}, bf16[4112,128]{1,0:T(8,128)(2,1)S(1)}, u32[]{:S(2)}, u32[]{:S(2)}) collective-permute-start(bf16[4112,128]{1,0:T(8,128)(2,1)S(1)} %copy-done.5), channel_id=1, source_target_pairs={{0,9},{1,13},{2,11},{3,15},{4,8},{5,12},{6,10},{7,14},{8,1},{9,5},... | collective-permute-start | bytes 3158024 | tf_op jit(solution)/shard_map/ppermute | solution.py:487
  34.4 57.3 %collective-permute-start.3 = (bf16[4112,128]{1,0:T(8,128)(2,1)S(1)}, bf16[4112,128]{1,0:T(8,128)(2,1)S(1)}, u32[]{:S(2)}, u32[]{:S(2)}) collective-permute-start(bf16[4112,128]{1,0:T(8,128)(2,1)S(1)} %copy-done.4), channel_id=1, source_target_pairs={{0,17},{1,21},{2,19},{3,23},{4,16},{5,20},{6,18},{7,22},{8,25},{9,... | collective-permute-start | bytes 3158024 | tf_op jit(solution)/shard_map/ppermute | solution.py:487
  36.4 1.6 collective-permute-start.15
  36.9 5.9 %copy-start.3 = (bf16[4112,128]{1,0:T(8,128)(2,1)S(1)}, bf16[4112,128]{1,0:T(8,128)(2,1)}, u32[]{:S(2)}) copy-start(bf16[4112,128]{1,0:T(8,128)(2,1)} %get-tuple-element.27) | copy-start | bytes 3158020
  38.1 1.6 collective-permute-start.14
  38.3 38.0 %copy-start.2 = (bf16[4112,128]{1,0:T(8,128)(2,1)S(1)}, bf16[4112,128]{1,0:T(8,128)(2,1)}, u32[]{:S(2)}) copy-start(bf16[4112,128]{1,0:T(8,128)(2,1)} %get-tuple-element.28) | copy-start | bytes 3158020
  39.7 1.6 collective-permute-start.13
  39.9 36.4 %copy-start.1 = (bf16[4112,128]{1,0:T(8,128)(2,1)S(1)}, bf16[4112,128]{1,0:T(8,128)(2,1)}, u32[]{:S(2)}) copy-start(bf16[4112,128]{1,0:T(8,128)(2,1)} %get-tuple-element.29) | copy-start | bytes 3158020
  40.0 47.0 %copy-start = (bf16[4112,128]{1,0:T(8,128)(2,1)S(1)}, bf16[4112,128]{1,0:T(8,128)(2,1)}, u32[]{:S(2)}) copy-start(bf16[4112,128]{1,0:T(8,128)(2,1)} %get-tuple-element.30) | copy-start | bytes 3158020
  41.2 1.6 collective-permute-start.12
  42.8 65.1 %collective-permute-start.4 = (bf16[4112,128]{1,0:T(8,128)(2,1)S(1)}, bf16[4112,128]{1,0:T(8,128)(2,1)S(1)}, u32[]{:S(2)}, u32[]{:S(2)}) collective-permute-start(bf16[4112,128]{1,0:T(8,128)(2,1)S(1)} %copy-done.3), channel_id=1, source_target_pairs={{0,24},{1,28},{2,26},{3,30},{4,25},{5,29},{6,27},{7,31},{8,16},{9,... | collective-permute-start | bytes 3158024 | tf_op jit(solution)/shard_map/ppermute | solution.py:487
  76.2 36.3 %collective-permute-start.5 = (bf16[4112,128]{1,0:T(8,128)(2,1)S(1)}, bf16[4112,128]{1,0:T(8,128)(2,1)S(1)}, u32[]{:S(2)}, u32[]{:S(2)}) collective-permute-start(bf16[4112,128]{1,0:T(8,128)(2,1)S(1)} %copy-done.2), channel_id=1, source_target_pairs={{0,25},{1,29},{2,27},{3,31},{4,24},{5,28},{6,26},{7,30},{8,17},{9,... | collective-permute-start | bytes 3158024 | tf_op jit(solution)/shard_map/ppermute | solution.py:487
  76.3 36.3 %collective-permute-start.6 = (bf16[4112,128]{1,0:T(8,128)(2,1)S(1)}, bf16[4112,128]{1,0:T(8,128)(2,1)S(1)}, u32[]{:S(2)}, u32[]{:S(2)}) collective-permute-start(bf16[4112,128]{1,0:T(8,128)(2,1)S(1)} %copy-done.1), channel_id=1, source_target_pairs={{0,0},{1,4},{2,2},{3,6},{4,1},{5,5},{6,3},{7,7},{8,8},{9,12},{10,1... | collective-permute-start | bytes 3158024 | tf_op jit(solution)/shard_map/ppermute | solution.py:487
  86.9 25.6 %collective-permute-start.7 = (bf16[4112,128]{1,0:T(8,128)(2,1)S(1)}, bf16[4112,128]{1,0:T(8,128)(2,1)S(1)}, u32[]{:S(2)}, u32[]{:S(2)}) collective-permute-start(bf16[4112,128]{1,0:T(8,128)(2,1)S(1)} %copy-done), channel_id=1, source_target_pairs={{0,1},{1,5},{2,3},{3,7},{4,0},{5,4},{6,2},{7,6},{8,9},{9,13},{10,1... | collective-permute-start | bytes 3158024 | tf_op jit(solution)/shard_map/ppermute | solution.py:487
  128.0 5.7 %collective-permute-start.16 = (bf16[1536,1024]{1,0:T(8,128)(2,1)S(1)}, bf16[1536,1024]{1,0:T(8,128)(2,1)S(1)}, u32[]{:S(2)}, u32[]{:S(2)}) collective-permute-start(bf16[1536,1024]{1,0:T(8,128)(2,1)S(1)} %couple.1.mine), channel_id=1, source_target_pairs={{0,4},{4,0},{8,12},{12,8},{16,20},{20,16},{24,28},{28,24},{1,5},{5... | collective-permute-start | bytes 9437192 | tf_op jit(solution)/shard_map/ppermute | solution.py:510
  136.0 11.5 %collective-permute-start.18 = (bf16[384,384]{1,0:T(8,128)(2,1)S(1)}, bf16[384,384]{1,0:T(8,128)(2,1)S(1)}, u32[]{:S(2)}, u32[]{:S(2)}) collective-permute-start(bf16[384,384]{1,0:T(8,128)(2,1)S(1)} %get-tuple-element.33), channel_id=1, source_target_pairs={{2,0},{3,4},{6,2},{7,6},{10,8},{11,12},{14,10},{15,14},{18,16},{19... | collective-permute-start | bytes 884744 | tf_op jit(solution)/shard_map/ppermute | solution.py:522
  137.3 10.2 %collective-permute-start.17 = (bf16[384,384]{1,0:T(8,128)(2,1)S(1)}, bf16[384,384]{1,0:T(8,128)(2,1)S(1)}, u32[]{:S(2)}, u32[]{:S(2)}) collective-permute-start(bf16[384,384]{1,0:T(8,128)(2,1)S(1)} %get-tuple-element.33), channel_id=1, source_target_pairs={{0,0},{1,4},{4,2},{5,6},{8,8},{9,12},{12,10},{13,14},{16,16},{17,2... | collective-permute-start | bytes 884744 | tf_op jit(solution)/shard_map/ppermute | solution.py:522
  141.0 44.5 %collective-permute-start.23 = (bf16[384,768]{1,0:T(8,128)(2,1)S(1)}, bf16[384,768]{1,0:T(8,128)(2,1)S(1)}, u32[]{:S(2)}, u32[]{:S(2)}) collective-permute-start(bf16[384,768]{1,0:T(8,128)(2,1)S(1)} %get-tuple-element.40), channel_id=1, source_target_pairs={{0,1},{1,5},{2,0},{3,4},{4,3},{5,7},{6,2},{7,6},{8,9},{9,13},{10,8... | collective-permute-start | bytes 1769480 | tf_op jit(solution)/shard_map/ppermute | solution.py:522
  146.8 38.7 %collective-permute-start.22 = (bf16[384,768]{1,0:T(8,128)(2,1)S(1)}, bf16[384,768]{1,0:T(8,128)(2,1)S(1)}, u32[]{:S(2)}, u32[]{:S(2)}) collective-permute-start(bf16[384,768]{1,0:T(8,128)(2,1)S(1)} %get-tuple-element.39), channel_id=1, source_target_pairs={{0,0},{1,4},{2,1},{3,5},{4,2},{5,6},{6,3},{7,7},{8,8},{9,12},{10,9... | collective-permute-start | bytes 1769480 | tf_op jit(solution)/shard_map/ppermute | solution.py:522
  147.6 35.9 %collective-permute-start.19 = (bf16[384,384]{1,0:T(8,128)(2,1)S(1)}, bf16[384,384]{1,0:T(8,128)(2,1)S(1)}, u32[]{:S(2)}, u32[]{:S(2)}) collective-permute-start(bf16[384,384]{1,0:T(8,128)(2,1)S(1)} %get-tuple-element.57), channel_id=1, source_target_pairs={{0,1},{2,3},{4,5},{6,7},{8,9},{10,11},{12,13},{14,15},{16,17},{18,... | collective-permute-start | bytes 884744 | tf_op jit(solution)/shard_map/ppermute | solution.py:535
  164.8 3.4 %collective-permute-start.20 = (bf16[768,128]{1,0:T(8,128)(2,1)S(1)}, bf16[768,128]{1,0:T(8,128)(2,1)S(1)}, u32[]{:S(2)}, u32[]{:S(2)}) collective-permute-start(bf16[768,128]{1,0:T(8,128)(2,1)S(1)} %get-tuple-element.37), channel_id=1, source_target_pairs={{0,0},{1,4},{2,1},{3,5},{4,2},{5,6},{6,3},{7,7},{8,8},{9,12},{10,9... | collective-permute-start | bytes 589832 | tf_op jit(solution)/shard_map/ppermute | solution.py:522
  165.5 18.0 %collective-permute-start.21 = (bf16[768,128]{1,0:T(8,128)(2,1)S(1)}, bf16[768,128]{1,0:T(8,128)(2,1)S(1)}, u32[]{:S(2)}, u32[]{:S(2)}) collective-permute-start(bf16[768,128]{1,0:T(8,128)(2,1)S(1)} %get-tuple-element.38), channel_id=1, source_target_pairs={{0,1},{1,5},{2,0},{3,4},{4,3},{5,7},{6,2},{7,6},{8,9},{9,13},{10,8... | collective-permute-start | bytes 589832 | tf_op jit(solution)/shard_map/ppermute | solution.py:522

commit v2 on v1

--- a/solution.py
+++ b/solution.py
@@ -253,131 +253,77 @@
     return lax.dot_general(left, right, (((1,), (1,)), ((), ())), preferred_element_type=jnp.float32)
 
 
-def load_halves(theirs, near, far, sems):
-    half = near.shape[0]
-    core = lax.axis_index("blk") % 2
-    copies = []
-    for at, (target, which) in enumerate(((near, core), (far, 1 - core))):
-        rows = pl.ds(pl.multiple_of(which * half, half), half)
-        copies.append(pltpu.make_async_copy(theirs.at[rows], target, sems.at[at]))
-        copies[-1].start()
-    return copies
-
-
-def message_rows(near, message, piece):
-    turn = (lax.axis_index("virt") // 2 + message) % 2
-    return near[pl.ds(pl.multiple_of(turn * piece, piece), piece), :]
+def half_of(array, which):
+    half = array.shape[0] // 2
+    return array[pl.ds(pl.multiple_of(which * half, half), half), :]
+
+
+def message_rows(array, message, piece):
+    start = lax.axis_index("blk") % 2 * (array.shape[0] // 2) + (lax.axis_index("virt") // 2 + message) % 2 * piece
+    return array[pl.ds(pl.multiple_of(start, piece), piece), :]
+
+
+def between_rows(array, piece):
+    near = half_of(array, lax.axis_index("blk") % 2)
+    return rows_times_rows(near[:piece, :], near[piece:, :])
+
+
+def across_rows(array, message, piece):
+    return rows_times_rows(message_rows(array, message, piece), half_of(array, 1 - lax.axis_index("blk") % 2))
 
 
 def own_join_kernel(piece, mine, between, *rest):
-    acrosses, corners, (near, far, sems) = rest[:2], rest[2:4], rest[4:]
-    copies = load_halves(mine, near, far, sems)
-    copies[0].wait()
-    between[...] = rows_times_rows(near[:piece, :], near[piece:, :])
+    acrosses, corners = rest[:2], rest[2:4]
+    between[...] = between_rows(mine, piece)
     for message in range(2):
-        rows = message_rows(near, message, piece)
+        rows = message_rows(mine, message, piece)
         corners[message][...] = rows_times_rows(rows, rows)
-    copies[1].wait()
+        acrosses[message][...] = across_rows(mine, message, piece)
+
+
+def first_join_kernel(piece, theirs, between_part, across_part, between, across):
+    between[...] = (between_part[...] + between_rows(theirs, piece)).astype(jnp.bfloat16)
+    across[...] = (across_part[...] + across_rows(theirs, 0, piece)).astype(jnp.bfloat16)
+
+
+def second_join_kernel(piece, edge, theirs, across_part, *rest):
+    corner_parts, (across, *corners) = rest[:2], rest[2:5]
     for message in range(2):
-        acrosses[message][...] = rows_times_rows(message_rows(near, message, piece), far[...])
-
-
-def own_join(mine, piece):
-    half = mine.shape[0] // 2
-    square, wide = (jax.ShapeDtypeStruct((piece, width), jnp.float32) for width in (piece, half))
-    return pl.pallas_call(
-        functools.partial(own_join_kernel, piece),
-        out_shape=[square, wide, wide, square, square],
-        in_specs=[pl.BlockSpec(memory_space=pl.ANY)],
-        out_specs=[pl.BlockSpec(memory_space=pltpu.VMEM)] * 5,
-        scratch_shapes=[
-            pltpu.VMEM((half, mine.shape[1]), jnp.bfloat16),
-            pltpu.VMEM((half, mine.shape[1]), jnp.bfloat16),
-            pltpu.SemaphoreType.DMA((2,)),
-        ],
-        compiler_params=pltpu.CompilerParams(vmem_limit_bytes=20 * 1024 * 1024),
-        name="own_join",
-    )(mine)
-
-
-def first_join_kernel(piece, theirs, between_part, across_part, between, across, near, far, held_b, held_a, sems):
-    copies = load_halves(theirs, near, far, sems)
-    for at, (ref, target) in enumerate(((between_part, held_b), (across_part, held_a))):
-        copies.append(pltpu.make_async_copy(ref, target, sems.at[2 + at]))
-        copies[-1].start()
-    copies[0].wait()
-    copies[2].wait()
-    between[...] = (held_b[...] + rows_times_rows(near[:piece, :], near[piece:, :])).astype(jnp.bfloat16)
-    copies[1].wait()
-    copies[3].wait()
-    across[...] = (held_a[...] + rows_times_rows(message_rows(near, 0, piece), far[...])).astype(jnp.bfloat16)
-
-
-def second_join_kernel(piece, edge, theirs, across_part, *rest):
-    corner_parts, (across, *corners), (near, far, held_a, *held_c, sems) = rest[:2], rest[2:5], rest[5:]
-    copies = load_halves(theirs, near, far, sems)
-    for at, (ref, target) in enumerate(zip((across_part, *corner_parts), (held_a, *held_c))):
-        copies.append(pltpu.make_async_copy(ref, target, sems.at[2 + at]))
-        copies[-1].start()
-    copies[0].wait()
-    for message in range(2):
-        copies[3 + message].wait()
-        rows = message_rows(near, message, piece)
-        block = held_c[message][...] + rows_times_rows(rows, rows)
+        rows = message_rows(theirs, message, piece)
+        block = corner_parts[message][...] + rows_times_rows(rows, rows)
         for at, (i, j) in enumerate(upper_blocks(piece // edge)):
             corners[message][at * edge : (at + 1) * edge, :] = block[
                 i * edge : (i + 1) * edge, j * edge : (j + 1) * edge
             ].astype(jnp.bfloat16)
-    copies[1].wait()
-    copies[2].wait()
-    across[...] = (held_a[...] + rows_times_rows(message_rows(near, 1, piece), far[...])).astype(jnp.bfloat16)
+    across[...] = (across_part[...] + across_rows(theirs, 1, piece)).astype(jnp.bfloat16)
+
+
+def join(kernel, shapes, operands):
+    return pl.pallas_call(
+        kernel,
+        out_shape=shapes,
+        in_specs=[pl.BlockSpec(memory_space=pltpu.VMEM)] * len(operands),
+        out_specs=[pl.BlockSpec(memory_space=pltpu.VMEM)] * len(shapes),
+        compiler_params=pltpu.CompilerParams(vmem_limit_bytes=28 * 1024 * 1024),
+    )(*operands)
+
+
+def own_join(mine, piece):
+    square, wide = (jax.ShapeDtypeStruct((piece, width), jnp.float32) for width in (piece, mine.shape[0] // 2))
+    return join(functools.partial(own_join_kernel, piece), [square, wide, wide, square, square], (mine,))
 
 
 def first_join(theirs, between_part, across_part, piece):
-    half = theirs.shape[0] // 2
-    return pl.pallas_call(
-        functools.partial(first_join_kernel, piece),
-        out_shape=[
-            jax.ShapeDtypeStruct((piece, piece), jnp.bfloat16),
-            jax.ShapeDtypeStruct((piece, half), jnp.bfloat16),
-        ],
-        in_specs=[pl.BlockSpec(memory_space=pl.ANY)] * 3,
-        out_specs=[pl.BlockSpec(memory_space=pltpu.VMEM)] * 2,
-        scratch_shapes=[
-            pltpu.VMEM((half, theirs.shape[1]), jnp.bfloat16),
-            pltpu.VMEM((half, theirs.shape[1]), jnp.bfloat16),
-            pltpu.VMEM((piece, piece), jnp.float32),
-            pltpu.VMEM((piece, half), jnp.float32),
-            pltpu.SemaphoreType.DMA((4,)),
-        ],
-        compiler_params=pltpu.CompilerParams(vmem_limit_bytes=20 * 1024 * 1024),
-        name="first_join",
-    )(theirs, between_part, across_part)
+    shapes = [jax.ShapeDtypeStruct((piece, width), jnp.bfloat16) for width in (piece, theirs.shape[0] // 2)]
+    operands = (theirs, between_part, across_part)
+    return join(functools.partial(first_join_kernel, piece), shapes, operands)
 
 
 def second_join(theirs, across_part, corner_part, other_corner_part, piece, edge):
-    half = theirs.shape[0] // 2
-    packed = (len(upper_blocks(piece // edge)) * edge, edge)
-    return pl.pallas_call(
-        functools.partial(second_join_kernel, piece, edge),
-        out_shape=[
-            jax.ShapeDtypeStruct((piece, half), jnp.bfloat16),
-            jax.ShapeDtypeStruct(packed, jnp.bfloat16),
-            jax.ShapeDtypeStruct(packed, jnp.bfloat16),
-        ],
-        in_specs=[pl.BlockSpec(memory_space=pl.ANY)] * 4,
-        out_specs=[pl.BlockSpec(memory_space=pltpu.VMEM)] * 3,
-        scratch_shapes=[
-            pltpu.VMEM((half, theirs.shape[1]), jnp.bfloat16),
-            pltpu.VMEM((half, theirs.shape[1]), jnp.bfloat16),
-            pltpu.VMEM((piece, half), jnp.float32),
-            pltpu.VMEM((piece, piece), jnp.float32),
-            pltpu.VMEM((piece, piece), jnp.float32),
-            pltpu.SemaphoreType.DMA((5,)),
-        ],
-        compiler_params=pltpu.CompilerParams(vmem_limit_bytes=20 * 1024 * 1024),
-        name="second_join",
-    )(theirs, across_part, corner_part, other_corner_part)
+    packed = jax.ShapeDtypeStruct((len(upper_blocks(piece // edge)) * edge, edge), jnp.bfloat16)
+    shapes = [jax.ShapeDtypeStruct((piece, theirs.shape[0] // 2), jnp.bfloat16), packed, packed]
+    operands = (theirs, across_part, corner_part, other_corner_part)
+    return join(functools.partial(second_join_kernel, piece, edge), shapes, operands)
 
 
 def near_kernel(piece, edge, factor, link, passed, corner, other_corner, result, made, *rest):
@@ -422,19 +368,11 @@
     copy.wait()
 
 
-def far_kernel(factor, begun, side, other_side, result, made, side_h, other_side_h, sems):
+def far_kernel(factor, begun, side, other_side, result, made, sem):
     half = made.shape[1]
-    copies = [
-        pltpu.make_async_copy(ref, target, sems.at[at])
-        for at, (ref, target) in enumerate(((side, side_h), (other_side, other_side_h)))
-    ]
-    for copy in copies:
-        copy.start()
-    for copy in copies:
-        copy.wait()
-    made[...] = (side_h[...].astype(jnp.float32) + other_side_h[...].astype(jnp.float32)) * factor
+    made[...] = (side[...].astype(jnp.float32) + other_side[...].astype(jnp.float32)) * factor
     columns = pl.ds(pl.multiple_of((1 - lax.axis_index("virt") // 2) * half, half), half)
-    copy = pltpu.make_async_copy(made, result.at[:, columns], sems.at[2])
+    copy = pltpu.make_async_copy(made, result.at[:, columns], sem)
     copy.start()
     copy.wait()
 
@@ -457,12 +395,10 @@
     return pl.pallas_call(
         functools.partial(far_kernel, factor),
         out_shape=result,
-        in_specs=[anywhere] * 3,
+        in_specs=[anywhere] + [pl.BlockSpec(memory_space=pltpu.VMEM)] * 2,
         out_specs=anywhere,
         input_output_aliases={0: 0},
-        scratch_shapes=[pltpu.VMEM((piece, half), jnp.float32)]
-        + [pltpu.VMEM(array.shape, array.dtype) for array in sides]
-        + [pltpu.SemaphoreType.DMA((3,))],
+        scratch_shapes=[pltpu.VMEM((piece, half), jnp.float32), pltpu.SemaphoreType.DMA],
         compiler_params=pltpu.CompilerParams(vmem_limit_bytes=20 * 1024 * 1024),
         name="far_half",
     )(begun, *sides)

time: 187 us -> 185 us (0.989)
  Pallas kernels: 34.3 us -> 31.1 us
    pallas_call x3, Pallas kernels: 8.34 us -> 5.46 us  [join(): pl.pallas_call(kernel, out_shape=shapes, in_specs=[pl.BlockSpec(memory_sp...]
  transfers between devices with their start and end apart: 24 -> 24, of which waited for: 12 -> 12; matrix products, arithmetic and copies ran while one was open for 1% -> 1% of each run, Pallas kernels for 7% -> 6%
where the time goes in v2:
time: 185 us
  waiting for transfers between devices  102 us (55%)
  starting transfers between devices  47.2 us (26%)
  Pallas kernels  31.1 us (17%)
  other arithmetic  2.76 us (1%)
    ppermute x8, waiting for transfers between devices, per_device(): sent.append(lax.ppermute(message, AXES, pairs))  65.2 us
    ppermute x1, starting transfers between devices, per_device(): passed = lax.ppermute(link.astype(jnp.bfloat16), AXES, on)  18.6 us
    ppermute x4, waiting for transfers between devices, per_device(): own.append(lax.ppermute(window, AXES, pairs))  15.4 us
    pallas_call x1, Pallas kernels, couple(): pl.pallas_call(functools.partial(couple_kernel, count, slots, edge), out_...  15.4 us
    ppermute x6, waiting for transfers between devices, sent_to(): return lax.ppermute(array, AXES, pairs)  14.2 us
    ppermute x6, starting transfers between devices, sent_to(): return lax.ppermute(array, AXES, pairs)  11.9 us
    ppermute x8, starting transfers between devices, per_device(): sent.append(lax.ppermute(message, AXES, pairs))  9.09 us
    ppermute x4, starting transfers between devices, per_device(): own.append(lax.ppermute(window, AXES, pairs))  6.68 us
  transfers between devices with their start and end apart: 24, of which 12 were waited for; matrix products, arithmetic and copies ran while one was open for 1% of the time, Pallas kernels for 6%

profile of v2, /device:TPU:0, one launch (start us, length us, event | category | flops | bytes accessed | tf_op | source)
XLA Modules:
  0.0 184.6 jit_solution(11797757218636136612)
XLA Ops:
  0.7 2.2 %window.1 = s16[128,1152]{1,0:T(8,128)(2,1)} custom-call(s32[1]{0:T(128)S(6)} %copy.9.start, f32[128,8192]{1,0:T(8,128)} %green.1), custom_call_target="tpu_custom_call" | custom-call | tf_op jit(solution)/shard_map/window/pallas_call | solution.py:233
  2.8 3.0 %collective-permute-start.8 = (s16[128,1152]{1,0:T(8,128)(2,1)}, s16[128,1152]{1,0:T(8,128)(2,1)S(1)}, u32[]{:S(2)}, u32[]{:S(2)}) collective-permute-start(s16[128,1152]{1,0:T(8,128)(2,1)} %window.1), channel_id=1, source_target_pairs={{0,16},{1,13},{2,18},{3,15},{4,20},{5,17},{6,22},{7,19},{8,24},{9,... | collective-permute-start | bytes 884744 | tf_op jit(solution)/shard_map/ppermute | solution.py:434
  5.9 1.4 collective-permute-start.11
  7.3 1.6 collective-permute-start.10
  8.9 0.6 collective-permute-start.9
  9.5 5.0 %pack.1 = (bf16[4112,128]{1,0:T(8,128)(2,1)}, bf16[4112,128]{1,0:T(8,128)(2,1)}, bf16[4112,128]{1,0:T(8,128)(2,1)}, bf16[4112,128]{1,0:T(8,128)(2,1)}, bf16[4112...) custom-call(s32[128]{0:T(128)} %bitcast.4, ...), custom_call_target="tpu_custom_call" | custom-call | tf_op jit(solution)/shard_map/pack/pallas_call | solution.py:111
  14.5 2.5 %collective-permute-start = (bf16[4112,128]{1,0:T(8,128)(2,1)}, bf16[4112,128]{1,0:T(8,128)(2,1)S(1)}, u32[]{:S(2)}, u32[]{:S(2)}) collective-permute-start(bf16[4112,128]{1,0:T(8,128)(2,1)} %get-tuple-element.23), channel_id=1, source_target_pairs={{0,8},{1,12},{2,10},{3,14},{4,9},{5,13},{6,11},{7,15},{8,0},{9,4},... | collective-permute-start | bytes 3158024 | tf_op jit(solution)/shard_map/ppermute | solution.py:423
  17.0 0.5 collective-permute-start.1
  17.7 0.2 fusion
  17.9 15.4 %collective-permute-done.9 = s16[128,1152]{1,0:T(8,128)(2,1)S(1)} collective-permute-done((s16[128,1152]{1,0:T(8,128)(2,1)}, s16[128,1152]{1,0:T(8,128)(2,1)S(1)}, u32[]{:S(2)}, u32[]{:S(2)}) %collective-permute-start.9) | collective-permute-done | bytes 294944 | tf_op jit(solution)/shard_map/ppermute | solution.py:434
  33.3 0.7 collective-permute-start.2
  34.2 0.2 fusion.1
  34.4 1.7 collective-permute-start.3
  36.3 0.2 fusion.2
  36.4 0.3 collective-permute-start.15
  36.9 0.1 fusion.3
  37.1 1.0 collective-permute-done.15
  38.1 0.2 collective-permute-start.14
  38.4 1.3 collective-permute-done.14
  39.7 0.2 collective-permute-start.13
  40.0 1.3 collective-permute-done.13
  41.2 0.2 collective-permute-start.12
  41.9 0.9 collective-permute-done.12
  42.8 2.5 %collective-permute-start.4 = (bf16[4112,128]{1,0:T(8,128)(2,1)S(1)}, bf16[4112,128]{1,0:T(8,128)(2,1)S(1)}, u32[]{:S(2)}, u32[]{:S(2)}) collective-permute-start(bf16[4112,128]{1,0:T(8,128)(2,1)S(1)} %copy-done.3), channel_id=1, source_target_pairs={{0,24},{1,28},{2,26},{3,30},{4,25},{5,29},{6,27},{7,31},{8,16},{9,... | collective-permute-start | bytes 3158024 | tf_op jit(solution)/shard_map/ppermute | solution.py:423
  45.4 30.8 %collective-permute-done.rest_0_ = bf16[4112,128]{1,0:T(8,128)(2,1)S(1)} collective-permute-done((bf16[4112,128]{1,0:T(8,128)(2,1)}, bf16[4112,128]{1,0:T(8,128)(2,1)S(1)}, u32[]{:S(2)}, u32[]{:S(2)}) %collective-permute-start) | collective-permute-done | bytes 1052704 | tf_op jit(solution)/shard_map/ppermute | solution.py:423
  76.3 0.7 collective-permute-start.6
  77.0 9.9 %collective-permute-done.2.rest_2_ = bf16[4112,128]{1,0:T(8,128)(2,1)S(1)} collective-permute-done((bf16[4112,128]{1,0:T(8,128)(2,1)S(1)}, bf16[4112,128]{1,0:T(8,128)(2,1)S(1)}, u32[]{:S(2)}, u32[]{:S(2)}) %collective-permute-start.2) | collective-permute-done | bytes 1052704 | tf_op jit(solution)/shard_map/ppermute | solution.py:423
  86.9 0.5 collective-permute-start.7
  87.5 0.1 fusion.7
  88.0 0.1 fusion.4
  88.1 3.5 %collective-permute-done.3.rest_3_ = bf16[4112,128]{1,0:T(8,128)(2,1)S(1)} collective-permute-done((bf16[4112,128]{1,0:T(8,128)(2,1)S(1)}, bf16[4112,128]{1,0:T(8,128)(2,1)S(1)}, u32[]{:S(2)}, u32[]{:S(2)}) %collective-permute-start.3) | collective-permute-done | bytes 1052704 | tf_op jit(solution)/shard_map/ppermute | solution.py:423
  91.7 16.3 %collective-permute-done.4.rest_4_ = bf16[4112,128]{1,0:T(8,128)(2,1)S(1)} collective-permute-done((bf16[4112,128]{1,0:T(8,128)(2,1)S(1)}, bf16[4112,128]{1,0:T(8,128)(2,1)S(1)}, u32[]{:S(2)}, u32[]{:S(2)}) %collective-permute-start.4) | collective-permute-done | bytes 1052704 | tf_op jit(solution)/shard_map/ppermute | solution.py:423
  108.0 4.6 %collective-permute-done.5.rest_5_ = bf16[4112,128]{1,0:T(8,128)(2,1)S(1)} collective-permute-done((bf16[4112,128]{1,0:T(8,128)(2,1)S(1)}, bf16[4112,128]{1,0:T(8,128)(2,1)S(1)}, u32[]{:S(2)}, u32[]{:S(2)}) %collective-permute-start.5) | collective-permute-done | bytes 1052704 | tf_op jit(solution)/shard_map/ppermute | solution.py:423
  112.6 15.4 %couple.1.mine = bf16[1536,1024]{1,0:T(8,128)(2,1)S(1)} custom-call(bf16[4112,128]{1,0:T(8,128)(2,1)S(1)} %collective-permute-done.rest_0_, bf16[4112,128]{1,0:T(8,128)(2,1)S(1)} %collective-permute-done.1.rest_1_, bf16[4112,128]{1,0:T(8,128)(2,1)S(1)} %collective-permute-done.2.rest_2_, bf16[4112,128]{1,0:T(8,128)(2,1)S(1)} %collective-permute-done.3.rest_3_, ...), custom_call_target="tpu_custom_call" | custom-call | tf_op jit(solution)/shard_map/couple/pallas_call | solution.py:193
  128.1 2.6 %shard_map.64 = (f32[384,384]{1,0:T(8,128)S(1)}, f32[384,768]{1,0:T(8,128)S(1)}, f32[384,768]{1,0:T(8,128)S(1)}, f32[384,384]{1,0:T(8,128)S(1)}, f32[384,384]{1,0:T(8,128)S(1)}) custom-call(bf16[1536,1024]{1,0:T(8,128)(2,1)S(1)} %couple.1.mine), custom_call_target="tpu_custom_call" | custom-call | tf_op jit(solution)/shard_map/pallas_call | solution.py:302
  130.7 3.0 %collective-permute-done.16.theirs = bf16[1536,1024]{1,0:T(8,128)(2,1)S(1)} collective-permute-done((bf16[1536,1024]{1,0:T(8,128)(2,1)S(1)}, bf16[1536,1024]{1,0:T(8,128)(2,1)S(1)}, u32[]{:S(2)}, u32[]{:S(2)}) %collective-permute-start.16) | collective-permute-done | bytes 3145760 | tf_op jit(solution)/shard_map/ppermute | solution.py:446
  133.7 1.2 shard_map.65
  134.9 1.3 collective-permute-start.18
  136.2 0.7 collective-permute-start.17
  136.9 1.6 shard_map.66
  138.5 5.8 %collective-permute-start.23 = (bf16[384,768]{1,0:T(8,128)(2,1)S(1)}, bf16[384,768]{1,0:T(8,128)(2,1)S(1)}, u32[]{:S(2)}, u32[]{:S(2)}) collective-permute-start(bf16[384,768]{1,0:T(8,128)(2,1)S(1)} %get-tuple-element.40), channel_id=1, source_target_pairs={{0,1},{1,5},{2,0},{3,4},{4,3},{5,7},{6,2},{7,6},{8,9},{9,13},{10,8... | collective-permute-start | bytes 1769480 | tf_op jit(solution)/shard_map/ppermute | solution.py:458
  144.4 0.7 collective-permute-start.22
  145.2 18.6 %collective-permute-start.19 = (bf16[384,384]{1,0:T(8,128)(2,1)S(1)}, bf16[384,384]{1,0:T(8,128)(2,1)S(1)}, u32[]{:S(2)}, u32[]{:S(2)}) collective-permute-start(bf16[384,384]{1,0:T(8,128)(2,1)S(1)} %get-tuple-element.57), channel_id=1, source_target_pairs={{0,1},{2,3},{4,5},{6,7},{8,9},{10,11},{12,13},{14,15},{16,17},{18,... | collective-permute-start | bytes 884744 | tf_op jit(solution)/shard_map/ppermute | solution.py:471
  163.7 0.7 collective-permute-start.20
  164.4 2.7 %collective-permute-start.21 = (bf16[768,128]{1,0:T(8,128)(2,1)S(1)}, bf16[768,128]{1,0:T(8,128)(2,1)S(1)}, u32[]{:S(2)}, u32[]{:S(2)}) collective-permute-start(bf16[768,128]{1,0:T(8,128)(2,1)S(1)} %get-tuple-element.38), channel_id=1, source_target_pairs={{0,1},{1,5},{2,0},{3,4},{4,3},{5,7},{6,2},{7,6},{8,9},{9,13},{10,8... | collective-permute-start | bytes 589832 | tf_op jit(solution)/shard_map/ppermute | solution.py:458
  167.2 14.2 %collective-permute-done.21.other_corner = bf16[768,128]{1,0:T(8,128)(2,1)S(1)} collective-permute-done((bf16[768,128]{1,0:T(8,128)(2,1)S(1)}, bf16[768,128]{1,0:T(8,128)(2,1)S(1)}, u32[]{:S(2)}, u32[]{:S(2)}) %collective-permute-start.21) | collective-permute-done | bytes 196640 | tf_op jit(solution)/shard_map/ppermute | solution.py:458
  181.3 1.9 %near_half.1.begun = f32[384,1536]{1,0:T(8,128)} custom-call(f32[384,384]{1,0:T(8,128)S(1)} %get-tuple-element.58.link, bf16[384,384]{1,0:T(8,128)(2,1)S(1)} %collective-permute-done.19.passed, bf16[768,128]{1,0:T(8,128)(2,1)S(1)} %collective-permute-done.20.corner, bf16[768,128]{1,0:T(8,128)(2,1)S(1)} %collective-permute-done.21.other_corner), custom_call_target="tpu_custom_call" | custom-call | tf_op jit(solution)/shard_map/near_half/pallas_call | solution.py:384
  183.3 1.2 far_half.1
  (45 shorter events, 2.0 us)
Async XLA Ops:
  2.8 14.2 %collective-permute-start.8 = (s16[128,1152]{1,0:T(8,128)(2,1)}, s16[128,1152]{1,0:T(8,128)(2,1)S(1)}, u32[]{:S(2)}, u32[]{:S(2)}) collective-permute-start(s16[128,1152]{1,0:T(8,128)(2,1)} %window.1), channel_id=1, source_target_pairs={{0,16},{1,13},{2,18},{3,15},{4,20},{5,17},{6,22},{7,19},{8,24},{9,... | collective-permute-start | bytes 884744 | tf_op jit(solution)/shard_map/ppermute | solution.py:434
  5.9 30.6 %collective-permute-start.11 = (s16[128,1152]{1,0:T(8,128)(2,1)}, s16[128,1152]{1,0:T(8,128)(2,1)S(1)}, u32[]{:S(2)}, u32[]{:S(2)}) collective-permute-start(s16[128,1152]{1,0:T(8,128)(2,1)} %window.1), channel_id=1, source_target_pairs={{0,24},{1,21},{2,26},{3,23},{4,28},{5,25},{6,30},{7,27},{8,0},{9,2... | collective-permute-start | bytes 884744 | tf_op jit(solution)/shard_map/ppermute | solution.py:434
  7.3 27.1 %collective-permute-start.10 = (s16[128,1152]{1,0:T(8,128)(2,1)}, s16[128,1152]{1,0:T(8,128)(2,1)S(1)}, u32[]{:S(2)}, u32[]{:S(2)}) collective-permute-start(s16[128,1152]{1,0:T(8,128)(2,1)} %window.1), channel_id=1, source_target_pairs={{0,0},{1,29},{2,2},{3,31},{4,4},{5,1},{6,6},{7,3},{8,8},{9,5},{10,... | collective-permute-start | bytes 884744 | tf_op jit(solution)/shard_map/ppermute | solution.py:434
  8.9 24.4 %collective-permute-start.9 = (s16[128,1152]{1,0:T(8,128)(2,1)}, s16[128,1152]{1,0:T(8,128)(2,1)S(1)}, u32[]{:S(2)}, u32[]{:S(2)}) collective-permute-start(s16[128,1152]{1,0:T(8,128)(2,1)} %window.1), channel_id=1, source_target_pairs={{0,8},{1,5},{2,10},{3,7},{4,12},{5,9},{6,14},{7,11},{8,16},{9,13},... | collective-permute-start | bytes 884744 | tf_op jit(solution)/shard_map/ppermute | solution.py:434
  14.5 18.8 %copy-start.5 = (bf16[4112,128]{1,0:T(8,128)(2,1)S(1)}, bf16[4112,128]{1,0:T(8,128)(2,1)}, u32[]{:S(2)}) copy-start(bf16[4112,128]{1,0:T(8,128)(2,1)} %get-tuple-element.25) | copy-start | bytes 3158020
  14.5 61.7 %collective-permute-start = (bf16[4112,128]{1,0:T(8,128)(2,1)}, bf16[4112,128]{1,0:T(8,128)(2,1)S(1)}, u32[]{:S(2)}, u32[]{:S(2)}) collective-permute-start(bf16[4112,128]{1,0:T(8,128)(2,1)} %get-tuple-element.23), channel_id=1, source_target_pairs={{0,8},{1,12},{2,10},{3,14},{4,9},{5,13},{6,11},{7,15},{8,0},{9,4},... | collective-permute-start | bytes 3158024 | tf_op jit(solution)/shard_map/ppermute | solution.py:423
  17.0 59.3 %collective-permute-start.1 = (bf16[4112,128]{1,0:T(8,128)(2,1)}, bf16[4112,128]{1,0:T(8,128)(2,1)S(1)}, u32[]{:S(2)}, u32[]{:S(2)}) collective-permute-start(bf16[4112,128]{1,0:T(8,128)(2,1)} %get-tuple-element.24), channel_id=1, source_target_pairs={{0,16},{1,20},{2,18},{3,22},{4,17},{5,21},{6,19},{7,23},{8,24},{9,... | collective-permute-start | bytes 3158024 | tf_op jit(solution)/shard_map/ppermute | solution.py:423
  17.9 16.5 %copy-start.4 = (bf16[4112,128]{1,0:T(8,128)(2,1)S(1)}, bf16[4112,128]{1,0:T(8,128)(2,1)}, u32[]{:S(2)}) copy-start(bf16[4112,128]{1,0:T(8,128)(2,1)} %get-tuple-element.26) | copy-start | bytes 3158020
  33.3 53.6 %collective-permute-start.2 = (bf16[4112,128]{1,0:T(8,128)(2,1)S(1)}, bf16[4112,128]{1,0:T(8,128)(2,1)S(1)}, u32[]{:S(2)}, u32[]{:S(2)}) collective-permute-start(bf16[4112,128]{1,0:T(8,128)(2,1)S(1)} %copy-done.5), channel_id=1, source_target_pairs={{0,9},{1,13},{2,11},{3,15},{4,8},{5,12},{6,10},{7,14},{8,1},{9,5},... | collective-permute-start | bytes 3158024 | tf_op jit(solution)/shard_map/ppermute | solution.py:423
  34.4 57.3 %collective-permute-start.3 = (bf16[4112,128]{1,0:T(8,128)(2,1)S(1)}, bf16[4112,128]{1,0:T(8,128)(2,1)S(1)}, u32[]{:S(2)}, u32[]{:S(2)}) collective-permute-start(bf16[4112,128]{1,0:T(8,128)(2,1)S(1)} %copy-done.4), channel_id=1, source_target_pairs={{0,17},{1,21},{2,19},{3,23},{4,16},{5,20},{6,18},{7,22},{8,25},{9,... | collective-permute-start | bytes 3158024 | tf_op jit(solution)/shard_map/ppermute | solution.py:423
  36.4 1.6 collective-permute-start.15
  36.9 5.9 %copy-start.3 = (bf16[4112,128]{1,0:T(8,128)(2,1)S(1)}, bf16[4112,128]{1,0:T(8,128)(2,1)}, u32[]{:S(2)}) copy-start(bf16[4112,128]{1,0:T(8,128)(2,1)} %get-tuple-element.27) | copy-start | bytes 3158020
  38.1 1.6 collective-permute-start.14
  38.3 38.0 %copy-start.2 = (bf16[4112,128]{1,0:T(8,128)(2,1)S(1)}, bf16[4112,128]{1,0:T(8,128)(2,1)}, u32[]{:S(2)}) copy-start(bf16[4112,128]{1,0:T(8,128)(2,1)} %get-tuple-element.28) | copy-start | bytes 3158020
  39.7 1.6 collective-permute-start.13
  39.9 36.4 %copy-start.1 = (bf16[4112,128]{1,0:T(8,128)(2,1)S(1)}, bf16[4112,128]{1,0:T(8,128)(2,1)}, u32[]{:S(2)}) copy-start(bf16[4112,128]{1,0:T(8,128)(2,1)} %get-tuple-element.29) | copy-start | bytes 3158020
  40.0 47.0 %copy-start = (bf16[4112,128]{1,0:T(8,128)(2,1)S(1)}, bf16[4112,128]{1,0:T(8,128)(2,1)}, u32[]{:S(2)}) copy-start(bf16[4112,128]{1,0:T(8,128)(2,1)} %get-tuple-element.30) | copy-start | bytes 3158020
  41.2 1.6 collective-permute-start.12
  42.8 65.1 %collective-permute-start.4 = (bf16[4112,128]{1,0:T(8,128)(2,1)S(1)}, bf16[4112,128]{1,0:T(8,128)(2,1)S(1)}, u32[]{:S(2)}, u32[]{:S(2)}) collective-permute-start(bf16[4112,128]{1,0:T(8,128)(2,1)S(1)} %copy-done.3), channel_id=1, source_target_pairs={{0,24},{1,28},{2,26},{3,30},{4,25},{5,29},{6,27},{7,31},{8,16},{9,... | collective-permute-start | bytes 3158024 | tf_op jit(solution)/shard_map/ppermute | solution.py:423
  76.2 36.3 %collective-permute-start.5 = (bf16[4112,128]{1,0:T(8,128)(2,1)S(1)}, bf16[4112,128]{1,0:T(8,128)(2,1)S(1)}, u32[]{:S(2)}, u32[]{:S(2)}) collective-permute-start(bf16[4112,128]{1,0:T(8,128)(2,1)S(1)} %copy-done.2), channel_id=1, source_target_pairs={{0,25},{1,29},{2,27},{3,31},{4,24},{5,28},{6,26},{7,30},{8,17},{9,... | collective-permute-start | bytes 3158024 | tf_op jit(solution)/shard_map/ppermute | solution.py:423
  76.3 36.3 %collective-permute-start.6 = (bf16[4112,128]{1,0:T(8,128)(2,1)S(1)}, bf16[4112,128]{1,0:T(8,128)(2,1)S(1)}, u32[]{:S(2)}, u32[]{:S(2)}) collective-permute-start(bf16[4112,128]{1,0:T(8,128)(2,1)S(1)} %copy-done.1), channel_id=1, source_target_pairs={{0,0},{1,4},{2,2},{3,6},{4,1},{5,5},{6,3},{7,7},{8,8},{9,12},{10,1... | collective-permute-start | bytes 3158024 | tf_op jit(solution)/shard_map/ppermute | solution.py:423
  86.9 25.6 %collective-permute-start.7 = (bf16[4112,128]{1,0:T(8,128)(2,1)S(1)}, bf16[4112,128]{1,0:T(8,128)(2,1)S(1)}, u32[]{:S(2)}, u32[]{:S(2)}) collective-permute-start(bf16[4112,128]{1,0:T(8,128)(2,1)S(1)} %copy-done), channel_id=1, source_target_pairs={{0,1},{1,5},{2,3},{3,7},{4,0},{5,4},{6,2},{7,6},{8,9},{9,13},{10,1... | collective-permute-start | bytes 3158024 | tf_op jit(solution)/shard_map/ppermute | solution.py:423
  128.0 5.7 %collective-permute-start.16 = (bf16[1536,1024]{1,0:T(8,128)(2,1)S(1)}, bf16[1536,1024]{1,0:T(8,128)(2,1)S(1)}, u32[]{:S(2)}, u32[]{:S(2)}) collective-permute-start(bf16[1536,1024]{1,0:T(8,128)(2,1)S(1)} %couple.1.mine), channel_id=1, source_target_pairs={{0,4},{4,0},{8,12},{12,8},{16,20},{20,16},{24,28},{28,24},{1,5},{5... | collective-permute-start | bytes 9437192 | tf_op jit(solution)/shard_map/ppermute | solution.py:446
  134.9 10.1 %collective-permute-start.18 = (bf16[384,384]{1,0:T(8,128)(2,1)S(1)}, bf16[384,384]{1,0:T(8,128)(2,1)S(1)}, u32[]{:S(2)}, u32[]{:S(2)}) collective-permute-start(bf16[384,384]{1,0:T(8,128)(2,1)S(1)} %get-tuple-element.33), channel_id=1, source_target_pairs={{2,0},{3,4},{6,2},{7,6},{10,8},{11,12},{14,10},{15,14},{18,16},{19... | collective-permute-start | bytes 884744 | tf_op jit(solution)/shard_map/ppermute | solution.py:458
  136.2 8.9 %collective-permute-start.17 = (bf16[384,384]{1,0:T(8,128)(2,1)S(1)}, bf16[384,384]{1,0:T(8,128)(2,1)S(1)}, u32[]{:S(2)}, u32[]{:S(2)}) collective-permute-start(bf16[384,384]{1,0:T(8,128)(2,1)S(1)} %get-tuple-element.33), channel_id=1, source_target_pairs={{0,0},{1,4},{4,2},{5,6},{8,8},{9,12},{12,10},{13,14},{16,16},{17,2... | collective-permute-start | bytes 884744 | tf_op jit(solution)/shard_map/ppermute | solution.py:458
  138.5 44.7 %collective-permute-start.23 = (bf16[384,768]{1,0:T(8,128)(2,1)S(1)}, bf16[384,768]{1,0:T(8,128)(2,1)S(1)}, u32[]{:S(2)}, u32[]{:S(2)}) collective-permute-start(bf16[384,768]{1,0:T(8,128)(2,1)S(1)} %get-tuple-element.40), channel_id=1, source_target_pairs={{0,1},{1,5},{2,0},{3,4},{4,3},{5,7},{6,2},{7,6},{8,9},{9,13},{10,8... | collective-permute-start | bytes 1769480 | tf_op jit(solution)/shard_map/ppermute | solution.py:458
  144.4 38.9 %collective-permute-start.22 = (bf16[384,768]{1,0:T(8,128)(2,1)S(1)}, bf16[384,768]{1,0:T(8,128)(2,1)S(1)}, u32[]{:S(2)}, u32[]{:S(2)}) collective-permute-start(bf16[384,768]{1,0:T(8,128)(2,1)S(1)} %get-tuple-element.39), channel_id=1, source_target_pairs={{0,0},{1,4},{2,1},{3,5},{4,2},{5,6},{6,3},{7,7},{8,8},{9,12},{10,9... | collective-permute-start | bytes 1769480 | tf_op jit(solution)/shard_map/ppermute | solution.py:458
  145.2 36.2 %collective-permute-start.19 = (bf16[384,384]{1,0:T(8,128)(2,1)S(1)}, bf16[384,384]{1,0:T(8,128)(2,1)S(1)}, u32[]{:S(2)}, u32[]{:S(2)}) collective-permute-start(bf16[384,384]{1,0:T(8,128)(2,1)S(1)} %get-tuple-element.57), channel_id=1, source_target_pairs={{0,1},{2,3},{4,5},{6,7},{8,9},{10,11},{12,13},{14,15},{16,17},{18,... | collective-permute-start | bytes 884744 | tf_op jit(solution)/shard_map/ppermute | solution.py:471
  163.7 3.4 %collective-permute-start.20 = (bf16[768,128]{1,0:T(8,128)(2,1)S(1)}, bf16[768,128]{1,0:T(8,128)(2,1)S(1)}, u32[]{:S(2)}, u32[]{:S(2)}) collective-permute-start(bf16[768,128]{1,0:T(8,128)(2,1)S(1)} %get-tuple-element.37), channel_id=1, source_target_pairs={{0,0},{1,4},{2,1},{3,5},{4,2},{5,6},{6,3},{7,7},{8,8},{9,12},{10,9... | collective-permute-start | bytes 589832 | tf_op jit(solution)/shard_map/ppermute | solution.py:458
  164.4 16.9 %collective-permute-start.21 = (bf16[768,128]{1,0:T(8,128)(2,1)S(1)}, bf16[768,128]{1,0:T(8,128)(2,1)S(1)}, u32[]{:S(2)}, u32[]{:S(2)}) collective-permute-start(bf16[768,128]{1,0:T(8,128)(2,1)S(1)} %get-tuple-element.38), channel_id=1, source_target_pairs={{0,1},{1,5},{2,0},{3,4},{4,3},{5,7},{6,2},{7,6},{8,9},{9,13},{10,8... | collective-permute-start | bytes 589832 | tf_op jit(solution)/shard_map/ppermute | solution.py:458

commit v3 on v2

--- a/solution.py
+++ b/solution.py
@@ -281,8 +281,11 @@
         acrosses[message][...] = across_rows(mine, message, piece)
 
 
-def first_join_kernel(piece, theirs, between_part, across_part, between, across):
+def between_kernel(piece, theirs, between_part, between):
     between[...] = (between_part[...] + between_rows(theirs, piece)).astype(jnp.bfloat16)
+
+
+def first_join_kernel(piece, theirs, across_part, across):
     across[...] = (across_part[...] + across_rows(theirs, 0, piece)).astype(jnp.bfloat16)
 
 
@@ -313,10 +316,14 @@
     return join(functools.partial(own_join_kernel, piece), [square, wide, wide, square, square], (mine,))
 
 
-def first_join(theirs, between_part, across_part, piece):
-    shapes = [jax.ShapeDtypeStruct((piece, width), jnp.bfloat16) for width in (piece, theirs.shape[0] // 2)]
-    operands = (theirs, between_part, across_part)
-    return join(functools.partial(first_join_kernel, piece), shapes, operands)
+def between_join(theirs, between_part, piece):
+    shapes = [jax.ShapeDtypeStruct((piece, piece), jnp.bfloat16)]
+    return join(functools.partial(between_kernel, piece), shapes, (theirs, between_part))[0]
+
+
+def first_join(theirs, across_part, piece):
+    shapes = [jax.ShapeDtypeStruct((piece, theirs.shape[0] // 2), jnp.bfloat16)]
+    return join(functools.partial(first_join_kernel, piece), shapes, (theirs, across_part))[0]
 
 
 def second_join(theirs, across_part, corner_part, other_corner_part, piece, edge):
@@ -446,7 +453,8 @@
     theirs = lax.ppermute(mine, "blk", swap)
     piece = PANEL // virt_count
     between, *parts = own_join(mine, piece)
-    between, across = first_join(theirs, between, parts[0], piece)
+    between = between_join(theirs, between, piece)
+    across = first_join(theirs, parts[0], piece)
     other_across, *corners = second_join(theirs, *parts[1:], piece, edge)
 
     def sent_to(array, message=None, group=None):
@@ -457,7 +465,9 @@
                 pairs.append((block * virt_count + virt, (2 * (block // 2) + virt % 2) * virt_count + row))
         return lax.ppermute(array, AXES, pairs)
 
-    links = [sent_to(between, group=group) for group in range(2)]
+    links = []
+    for group in range(2):
+        links.append(sent_to(between, group=group))
     sides = [sent_to(across, 0)]
     for message, corner in enumerate(corners):
         corners[message] = sent_to(corner, message)

time: 185 us -> 185 us (level)
    pallas_call x3 -> x4, Pallas kernels: 5.46 us -> 5.67 us  [join(): pl.pallas_call(kernel, out_shape=shapes, in_specs=[pl.BlockSpec(memory_sp...]
  transfers between devices with their start and end apart: 24 -> 24, of which waited for: 12 -> 12; matrix products, arithmetic and copies ran while one was open for 1% -> 2% of each run, Pallas kernels for 6% -> 7%
where the time goes in v3:
time: 185 us; the launch traced here: 184 us
  waiting for transfers between devices  102 us (55%)
  starting transfers between devices  46.4 us (25%)
  Pallas kernels  31.3 us (17%)
  other arithmetic  2.76 us (1%)
    ppermute x8, waiting for transfers between devices, per_device(): sent.append(lax.ppermute(message, AXES, pairs))  65.1 us
    ppermute x1, starting transfers between devices, per_device(): passed = lax.ppermute(link.astype(jnp.bfloat16), AXES, on)  17.7 us
    ppermute x4, waiting for transfers between devices, per_device(): own.append(lax.ppermute(window, AXES, pairs))  15.4 us
    pallas_call x1, Pallas kernels, couple(): pl.pallas_call(functools.partial(couple_kernel, count, slots, edge), out_...  15.4 us
    ppermute x6, waiting for transfers between devices, sent_to(): return lax.ppermute(array, AXES, pairs)  14.2 us
    ppermute x6, starting transfers between devices, sent_to(): return lax.ppermute(array, AXES, pairs)  11.9 us
    ppermute x8, starting transfers between devices, per_device(): sent.append(lax.ppermute(message, AXES, pairs))  9.18 us
    ppermute x4, starting transfers between devices, per_device(): own.append(lax.ppermute(window, AXES, pairs))  6.68 us
  transfers between devices with their start and end apart: 24, of which 12 were waited for; matrix products, arithmetic and copies ran while one was open for 2% of the time, Pallas kernels for 7%

profile of v3, /device:TPU:0, one launch (start us, length us, event | category | flops | bytes accessed | tf_op | source)
XLA Modules:
  0.0 184.0 jit_solution(2481860557905433974)
XLA Ops:
  0.7 2.2 %window.1 = s16[128,1152]{1,0:T(8,128)(2,1)} custom-call(s32[1]{0:T(128)S(6)} %copy.9.start, f32[128,8192]{1,0:T(8,128)} %green.1), custom_call_target="tpu_custom_call" | custom-call | tf_op jit(solution)/shard_map/window/pallas_call | solution.py:233
  2.8 3.0 %collective-permute-start.8 = (s16[128,1152]{1,0:T(8,128)(2,1)}, s16[128,1152]{1,0:T(8,128)(2,1)S(1)}, u32[]{:S(2)}, u32[]{:S(2)}) collective-permute-start(s16[128,1152]{1,0:T(8,128)(2,1)} %window.1), channel_id=1, source_target_pairs={{0,16},{1,13},{2,18},{3,15},{4,20},{5,17},{6,22},{7,19},{8,24},{9,... | collective-permute-start | bytes 884744 | tf_op jit(solution)/shard_map/ppermute | solution.py:441
  5.9 1.4 collective-permute-start.11
  7.3 1.6 collective-permute-start.10
  8.9 0.6 collective-permute-start.9
  9.5 5.0 %pack.1 = (bf16[4112,128]{1,0:T(8,128)(2,1)}, bf16[4112,128]{1,0:T(8,128)(2,1)}, bf16[4112,128]{1,0:T(8,128)(2,1)}, bf16[4112,128]{1,0:T(8,128)(2,1)}, bf16[4112...) custom-call(s32[128]{0:T(128)} %bitcast.4, ...), custom_call_target="tpu_custom_call" | custom-call | tf_op jit(solution)/shard_map/pack/pallas_call | solution.py:111
  14.6 2.4 %collective-permute-start = (bf16[4112,128]{1,0:T(8,128)(2,1)}, bf16[4112,128]{1,0:T(8,128)(2,1)S(1)}, u32[]{:S(2)}, u32[]{:S(2)}) collective-permute-start(bf16[4112,128]{1,0:T(8,128)(2,1)} %get-tuple-element.21), channel_id=1, source_target_pairs={{0,8},{1,12},{2,10},{3,14},{4,9},{5,13},{6,11},{7,15},{8,0},{9,4},... | collective-permute-start | bytes 3158024 | tf_op jit(solution)/shard_map/ppermute | solution.py:430
  17.0 0.5 collective-permute-start.1
  17.7 0.2 fusion
  17.9 15.4 %collective-permute-done.9 = s16[128,1152]{1,0:T(8,128)(2,1)S(1)} collective-permute-done((s16[128,1152]{1,0:T(8,128)(2,1)}, s16[128,1152]{1,0:T(8,128)(2,1)S(1)}, u32[]{:S(2)}, u32[]{:S(2)}) %collective-permute-start.9) | collective-permute-done | bytes 294944 | tf_op jit(solution)/shard_map/ppermute | solution.py:441
  33.3 0.7 collective-permute-start.2
  34.2 0.2 fusion.1
  34.4 1.7 collective-permute-start.3
  36.3 0.2 fusion.2
  36.4 0.3 collective-permute-start.15
  36.9 0.1 fusion.3
  37.0 1.0 collective-permute-done.15
  38.1 0.2 collective-permute-start.14
  38.4 1.3 collective-permute-done.14
  39.7 0.2 collective-permute-start.13
  40.0 1.3 collective-permute-done.13
  41.2 0.2 collective-permute-start.12
  41.9 0.9 collective-permute-done.12
  42.8 2.5 %collective-permute-start.4 = (bf16[4112,128]{1,0:T(8,128)(2,1)S(1)}, bf16[4112,128]{1,0:T(8,128)(2,1)S(1)}, u32[]{:S(2)}, u32[]{:S(2)}) collective-permute-start(bf16[4112,128]{1,0:T(8,128)(2,1)S(1)} %copy-done.3), channel_id=1, source_target_pairs={{0,24},{1,28},{2,26},{3,30},{4,25},{5,29},{6,27},{7,31},{8,16},{9,... | collective-permute-start | bytes 3158024 | tf_op jit(solution)/shard_map/ppermute | solution.py:430
  45.4 30.8 %collective-permute-done.rest_0_ = bf16[4112,128]{1,0:T(8,128)(2,1)S(1)} collective-permute-done((bf16[4112,128]{1,0:T(8,128)(2,1)}, bf16[4112,128]{1,0:T(8,128)(2,1)S(1)}, u32[]{:S(2)}, u32[]{:S(2)}) %collective-permute-start) | collective-permute-done | bytes 1052704 | tf_op jit(solution)/shard_map/ppermute | solution.py:430
  76.3 0.7 collective-permute-start.6
  77.0 9.9 %collective-permute-done.2.rest_2_ = bf16[4112,128]{1,0:T(8,128)(2,1)S(1)} collective-permute-done((bf16[4112,128]{1,0:T(8,128)(2,1)S(1)}, bf16[4112,128]{1,0:T(8,128)(2,1)S(1)}, u32[]{:S(2)}, u32[]{:S(2)}) %collective-permute-start.2) | collective-permute-done | bytes 1052704 | tf_op jit(solution)/shard_map/ppermute | solution.py:430
  86.9 0.6 collective-permute-start.7
  87.6 0.1 fusion.7
  88.2 3.5 %collective-permute-done.3.rest_3_ = bf16[4112,128]{1,0:T(8,128)(2,1)S(1)} collective-permute-done((bf16[4112,128]{1,0:T(8,128)(2,1)S(1)}, bf16[4112,128]{1,0:T(8,128)(2,1)S(1)}, u32[]{:S(2)}, u32[]{:S(2)}) %collective-permute-start.3) | collective-permute-done | bytes 1052704 | tf_op jit(solution)/shard_map/ppermute | solution.py:430
  91.7 16.3 %collective-permute-done.4.rest_4_ = bf16[4112,128]{1,0:T(8,128)(2,1)S(1)} collective-permute-done((bf16[4112,128]{1,0:T(8,128)(2,1)S(1)}, bf16[4112,128]{1,0:T(8,128)(2,1)S(1)}, u32[]{:S(2)}, u32[]{:S(2)}) %collective-permute-start.4) | collective-permute-done | bytes 1052704 | tf_op jit(solution)/shard_map/ppermute | solution.py:430
  107.9 4.6 %collective-permute-done.5.rest_5_ = bf16[4112,128]{1,0:T(8,128)(2,1)S(1)} collective-permute-done((bf16[4112,128]{1,0:T(8,128)(2,1)S(1)}, bf16[4112,128]{1,0:T(8,128)(2,1)S(1)}, u32[]{:S(2)}, u32[]{:S(2)}) %collective-permute-start.5) | collective-permute-done | bytes 1052704 | tf_op jit(solution)/shard_map/ppermute | solution.py:430
  112.6 15.4 %couple.1.mine = bf16[1536,1024]{1,0:T(8,128)(2,1)S(1)} custom-call(bf16[4112,128]{1,0:T(8,128)(2,1)S(1)} %collective-permute-done.rest_0_, bf16[4112,128]{1,0:T(8,128)(2,1)S(1)} %collective-permute-done.1.rest_1_, bf16[4112,128]{1,0:T(8,128)(2,1)S(1)} %collective-permute-done.2.rest_2_, bf16[4112,128]{1,0:T(8,128)(2,1)S(1)} %collective-permute-done.3.rest_3_, ...), custom_call_target="tpu_custom_call" | custom-call | tf_op jit(solution)/shard_map/couple/pallas_call | solution.py:193
  128.0 2.6 %shard_map.64 = (f32[384,384]{1,0:T(8,128)S(1)}, f32[384,768]{1,0:T(8,128)S(1)}, f32[384,768]{1,0:T(8,128)S(1)}, f32[384,384]{1,0:T(8,128)S(1)}, f32[384,384]{1,0:T(8,128)S(1)}) custom-call(bf16[1536,1024]{1,0:T(8,128)(2,1)S(1)} %couple.1.mine), custom_call_target="tpu_custom_call" | custom-call | tf_op jit(solution)/shard_map/pallas_call | solution.py:305
  130.7 3.0 %collective-permute-done.16.theirs = bf16[1536,1024]{1,0:T(8,128)(2,1)S(1)} collective-permute-done((bf16[1536,1024]{1,0:T(8,128)(2,1)S(1)}, bf16[1536,1024]{1,0:T(8,128)(2,1)S(1)}, u32[]{:S(2)}, u32[]{:S(2)}) %collective-permute-start.16) | collective-permute-done | bytes 3145760 | tf_op jit(solution)/shard_map/ppermute | solution.py:453
  133.7 0.6 shard_map.65
  134.3 1.3 collective-permute-start.18
  135.6 0.7 collective-permute-start.17
  136.3 1.6 shard_map.66
  137.9 5.8 %collective-permute-start.23 = (bf16[384,768]{1,0:T(8,128)(2,1)S(1)}, bf16[384,768]{1,0:T(8,128)(2,1)S(1)}, u32[]{:S(2)}, u32[]{:S(2)}) collective-permute-start(bf16[384,768]{1,0:T(8,128)(2,1)S(1)} %get-tuple-element.36), channel_id=1, source_target_pairs={{0,1},{1,5},{2,0},{3,4},{4,3},{5,7},{6,2},{7,6},{8,9},{9,13},{10,8... | collective-permute-start | bytes 1769480 | tf_op jit(solution)/shard_map/ppermute | solution.py:466
  143.7 0.8 shard_map.67
  144.6 0.7 collective-permute-start.22
  145.4 17.7 %collective-permute-start.19 = (bf16[384,384]{1,0:T(8,128)(2,1)S(1)}, bf16[384,384]{1,0:T(8,128)(2,1)S(1)}, u32[]{:S(2)}, u32[]{:S(2)}) collective-permute-start(bf16[384,384]{1,0:T(8,128)(2,1)S(1)} %get-tuple-element.53), channel_id=1, source_target_pairs={{0,1},{2,3},{4,5},{6,7},{8,9},{10,11},{12,13},{14,15},{16,17},{18,... | collective-permute-start | bytes 884744 | tf_op jit(solution)/shard_map/ppermute | solution.py:481
  163.1 0.7 collective-permute-start.20
  163.8 2.7 %collective-permute-start.21 = (bf16[768,128]{1,0:T(8,128)(2,1)S(1)}, bf16[768,128]{1,0:T(8,128)(2,1)S(1)}, u32[]{:S(2)}, u32[]{:S(2)}) collective-permute-start(bf16[768,128]{1,0:T(8,128)(2,1)S(1)} %get-tuple-element.34), channel_id=1, source_target_pairs={{0,1},{1,5},{2,0},{3,4},{4,3},{5,7},{6,2},{7,6},{8,9},{9,13},{10,8... | collective-permute-start | bytes 589832 | tf_op jit(solution)/shard_map/ppermute | solution.py:466
  166.5 14.2 %collective-permute-done.21.other_corner = bf16[768,128]{1,0:T(8,128)(2,1)S(1)} collective-permute-done((bf16[768,128]{1,0:T(8,128)(2,1)S(1)}, bf16[768,128]{1,0:T(8,128)(2,1)S(1)}, u32[]{:S(2)}, u32[]{:S(2)}) %collective-permute-start.21) | collective-permute-done | bytes 196640 | tf_op jit(solution)/shard_map/ppermute | solution.py:466
  180.7 1.9 %near_half.1.begun = f32[384,1536]{1,0:T(8,128)} custom-call(f32[384,384]{1,0:T(8,128)S(1)} %get-tuple-element.54.link, bf16[384,384]{1,0:T(8,128)(2,1)S(1)} %collective-permute-done.19.passed, bf16[768,128]{1,0:T(8,128)(2,1)S(1)} %collective-permute-done.20.corner, bf16[768,128]{1,0:T(8,128)(2,1)S(1)} %collective-permute-done.21.other_corner), custom_call_target="tpu_custom_call" | custom-call | tf_op jit(solution)/shard_map/near_half/pallas_call | solution.py:391
  182.7 1.2 far_half.1
  (46 shorter events, 2.2 us)
Async XLA Ops:
  2.8 14.2 %collective-permute-start.8 = (s16[128,1152]{1,0:T(8,128)(2,1)}, s16[128,1152]{1,0:T(8,128)(2,1)S(1)}, u32[]{:S(2)}, u32[]{:S(2)}) collective-permute-start(s16[128,1152]{1,0:T(8,128)(2,1)} %window.1), channel_id=1, source_target_pairs={{0,16},{1,13},{2,18},{3,15},{4,20},{5,17},{6,22},{7,19},{8,24},{9,... | collective-permute-start | bytes 884744 | tf_op jit(solution)/shard_map/ppermute | solution.py:441
  5.9 30.6 %collective-permute-start.11 = (s16[128,1152]{1,0:T(8,128)(2,1)}, s16[128,1152]{1,0:T(8,128)(2,1)S(1)}, u32[]{:S(2)}, u32[]{:S(2)}) collective-permute-start(s16[128,1152]{1,0:T(8,128)(2,1)} %window.1), channel_id=1, source_target_pairs={{0,24},{1,21},{2,26},{3,23},{4,28},{5,25},{6,30},{7,27},{8,0},{9,2... | collective-permute-start | bytes 884744 | tf_op jit(solution)/shard_map/ppermute | solution.py:441
  7.3 27.1 %collective-permute-start.10 = (s16[128,1152]{1,0:T(8,128)(2,1)}, s16[128,1152]{1,0:T(8,128)(2,1)S(1)}, u32[]{:S(2)}, u32[]{:S(2)}) collective-permute-start(s16[128,1152]{1,0:T(8,128)(2,1)} %window.1), channel_id=1, source_target_pairs={{0,0},{1,29},{2,2},{3,31},{4,4},{5,1},{6,6},{7,3},{8,8},{9,5},{10,... | collective-permute-start | bytes 884744 | tf_op jit(solution)/shard_map/ppermute | solution.py:441
  8.9 24.4 %collective-permute-start.9 = (s16[128,1152]{1,0:T(8,128)(2,1)}, s16[128,1152]{1,0:T(8,128)(2,1)S(1)}, u32[]{:S(2)}, u32[]{:S(2)}) collective-permute-start(s16[128,1152]{1,0:T(8,128)(2,1)} %window.1), channel_id=1, source_target_pairs={{0,8},{1,5},{2,10},{3,7},{4,12},{5,9},{6,14},{7,11},{8,16},{9,13},... | collective-permute-start | bytes 884744 | tf_op jit(solution)/shard_map/ppermute | solution.py:441
  14.5 18.7 %copy-start.5 = (bf16[4112,128]{1,0:T(8,128)(2,1)S(1)}, bf16[4112,128]{1,0:T(8,128)(2,1)}, u32[]{:S(2)}) copy-start(bf16[4112,128]{1,0:T(8,128)(2,1)} %get-tuple-element.23) | copy-start | bytes 3158020
  14.6 61.7 %collective-permute-start = (bf16[4112,128]{1,0:T(8,128)(2,1)}, bf16[4112,128]{1,0:T(8,128)(2,1)S(1)}, u32[]{:S(2)}, u32[]{:S(2)}) collective-permute-start(bf16[4112,128]{1,0:T(8,128)(2,1)} %get-tuple-element.21), channel_id=1, source_target_pairs={{0,8},{1,12},{2,10},{3,14},{4,9},{5,13},{6,11},{7,15},{8,0},{9,4},... | collective-permute-start | bytes 3158024 | tf_op jit(solution)/shard_map/ppermute | solution.py:430
  17.0 59.2 %collective-permute-start.1 = (bf16[4112,128]{1,0:T(8,128)(2,1)}, bf16[4112,128]{1,0:T(8,128)(2,1)S(1)}, u32[]{:S(2)}, u32[]{:S(2)}) collective-permute-start(bf16[4112,128]{1,0:T(8,128)(2,1)} %get-tuple-element.22), channel_id=1, source_target_pairs={{0,16},{1,20},{2,18},{3,22},{4,17},{5,21},{6,19},{7,23},{8,24},{9,... | collective-permute-start | bytes 3158024 | tf_op jit(solution)/shard_map/ppermute | solution.py:430
  17.9 16.5 %copy-start.4 = (bf16[4112,128]{1,0:T(8,128)(2,1)S(1)}, bf16[4112,128]{1,0:T(8,128)(2,1)}, u32[]{:S(2)}) copy-start(bf16[4112,128]{1,0:T(8,128)(2,1)} %get-tuple-element.24) | copy-start | bytes 3158020
  33.3 53.6 %collective-permute-start.2 = (bf16[4112,128]{1,0:T(8,128)(2,1)S(1)}, bf16[4112,128]{1,0:T(8,128)(2,1)S(1)}, u32[]{:S(2)}, u32[]{:S(2)}) collective-permute-start(bf16[4112,128]{1,0:T(8,128)(2,1)S(1)} %copy-done.5), channel_id=1, source_target_pairs={{0,9},{1,13},{2,11},{3,15},{4,8},{5,12},{6,10},{7,14},{8,1},{9,5},... | collective-permute-start | bytes 3158024 | tf_op jit(solution)/shard_map/ppermute | solution.py:430
  34.4 57.3 %collective-permute-start.3 = (bf16[4112,128]{1,0:T(8,128)(2,1)S(1)}, bf16[4112,128]{1,0:T(8,128)(2,1)S(1)}, u32[]{:S(2)}, u32[]{:S(2)}) collective-permute-start(bf16[4112,128]{1,0:T(8,128)(2,1)S(1)} %copy-done.4), channel_id=1, source_target_pairs={{0,17},{1,21},{2,19},{3,23},{4,16},{5,20},{6,18},{7,22},{8,25},{9,... | collective-permute-start | bytes 3158024 | tf_op jit(solution)/shard_map/ppermute | solution.py:430
  36.4 1.6 collective-permute-start.15
  36.9 5.9 %copy-start.3 = (bf16[4112,128]{1,0:T(8,128)(2,1)S(1)}, bf16[4112,128]{1,0:T(8,128)(2,1)}, u32[]{:S(2)}) copy-start(bf16[4112,128]{1,0:T(8,128)(2,1)} %get-tuple-element.25) | copy-start | bytes 3158020
  38.1 1.6 collective-permute-start.14
  38.3 38.0 %copy-start.2 = (bf16[4112,128]{1,0:T(8,128)(2,1)S(1)}, bf16[4112,128]{1,0:T(8,128)(2,1)}, u32[]{:S(2)}) copy-start(bf16[4112,128]{1,0:T(8,128)(2,1)} %get-tuple-element.26) | copy-start | bytes 3158020
  39.7 1.6 collective-permute-start.13
  39.9 36.4 %copy-start.1 = (bf16[4112,128]{1,0:T(8,128)(2,1)S(1)}, bf16[4112,128]{1,0:T(8,128)(2,1)}, u32[]{:S(2)}) copy-start(bf16[4112,128]{1,0:T(8,128)(2,1)} %get-tuple-element.27) | copy-start | bytes 3158020
  39.9 47.0 %copy-start = (bf16[4112,128]{1,0:T(8,128)(2,1)S(1)}, bf16[4112,128]{1,0:T(8,128)(2,1)}, u32[]{:S(2)}) copy-start(bf16[4112,128]{1,0:T(8,128)(2,1)} %get-tuple-element.28) | copy-start | bytes 3158020
  41.2 1.6 collective-permute-start.12
  42.8 65.1 %collective-permute-start.4 = (bf16[4112,128]{1,0:T(8,128)(2,1)S(1)}, bf16[4112,128]{1,0:T(8,128)(2,1)S(1)}, u32[]{:S(2)}, u32[]{:S(2)}) collective-permute-start(bf16[4112,128]{1,0:T(8,128)(2,1)S(1)} %copy-done.3), channel_id=1, source_target_pairs={{0,24},{1,28},{2,26},{3,30},{4,25},{5,29},{6,27},{7,31},{8,16},{9,... | collective-permute-start | bytes 3158024 | tf_op jit(solution)/shard_map/ppermute | solution.py:430
  76.2 36.3 %collective-permute-start.5 = (bf16[4112,128]{1,0:T(8,128)(2,1)S(1)}, bf16[4112,128]{1,0:T(8,128)(2,1)S(1)}, u32[]{:S(2)}, u32[]{:S(2)}) collective-permute-start(bf16[4112,128]{1,0:T(8,128)(2,1)S(1)} %copy-done.2), channel_id=1, source_target_pairs={{0,25},{1,29},{2,27},{3,31},{4,24},{5,28},{6,26},{7,30},{8,17},{9,... | collective-permute-start | bytes 3158024 | tf_op jit(solution)/shard_map/ppermute | solution.py:430
  76.3 36.3 %collective-permute-start.6 = (bf16[4112,128]{1,0:T(8,128)(2,1)S(1)}, bf16[4112,128]{1,0:T(8,128)(2,1)S(1)}, u32[]{:S(2)}, u32[]{:S(2)}) collective-permute-start(bf16[4112,128]{1,0:T(8,128)(2,1)S(1)} %copy-done.1), channel_id=1, source_target_pairs={{0,0},{1,4},{2,2},{3,6},{4,1},{5,5},{6,3},{7,7},{8,8},{9,12},{10,1... | collective-permute-start | bytes 3158024 | tf_op jit(solution)/shard_map/ppermute | solution.py:430
  86.9 25.7 %collective-permute-start.7 = (bf16[4112,128]{1,0:T(8,128)(2,1)S(1)}, bf16[4112,128]{1,0:T(8,128)(2,1)S(1)}, u32[]{:S(2)}, u32[]{:S(2)}) collective-permute-start(bf16[4112,128]{1,0:T(8,128)(2,1)S(1)} %copy-done), channel_id=1, source_target_pairs={{0,1},{1,5},{2,3},{3,7},{4,0},{5,4},{6,2},{7,6},{8,9},{9,13},{10,1... | collective-permute-start | bytes 3158024 | tf_op jit(solution)/shard_map/ppermute | solution.py:430
  128.0 5.7 %collective-permute-start.16 = (bf16[1536,1024]{1,0:T(8,128)(2,1)S(1)}, bf16[1536,1024]{1,0:T(8,128)(2,1)S(1)}, u32[]{:S(2)}, u32[]{:S(2)}) collective-permute-start(bf16[1536,1024]{1,0:T(8,128)(2,1)S(1)} %couple.1.mine), channel_id=1, source_target_pairs={{0,4},{4,0},{8,12},{12,8},{16,20},{20,16},{24,28},{28,24},{1,5},{5... | collective-permute-start | bytes 9437192 | tf_op jit(solution)/shard_map/ppermute | solution.py:453
  134.3 11.0 %collective-permute-start.18 = (bf16[384,384]{1,0:T(8,128)(2,1)S(1)}, bf16[384,384]{1,0:T(8,128)(2,1)S(1)}, u32[]{:S(2)}, u32[]{:S(2)}) collective-permute-start(bf16[384,384]{1,0:T(8,128)(2,1)S(1)} %shard_map.65), channel_id=1, source_target_pairs={{2,0},{3,4},{6,2},{7,6},{10,8},{11,12},{14,10},{15,14},{18,16},{19... | collective-permute-start | bytes 884744 | tf_op jit(solution)/shard_map/ppermute | solution.py:466
  135.6 9.7 %collective-permute-start.17 = (bf16[384,384]{1,0:T(8,128)(2,1)S(1)}, bf16[384,384]{1,0:T(8,128)(2,1)S(1)}, u32[]{:S(2)}, u32[]{:S(2)}) collective-permute-start(bf16[384,384]{1,0:T(8,128)(2,1)S(1)} %shard_map.65), channel_id=1, source_target_pairs={{0,0},{1,4},{4,2},{5,6},{8,8},{9,12},{12,10},{13,14},{16,16},{17,2... | collective-permute-start | bytes 884744 | tf_op jit(solution)/shard_map/ppermute | solution.py:466
  137.9 44.7 %collective-permute-start.23 = (bf16[384,768]{1,0:T(8,128)(2,1)S(1)}, bf16[384,768]{1,0:T(8,128)(2,1)S(1)}, u32[]{:S(2)}, u32[]{:S(2)}) collective-permute-start(bf16[384,768]{1,0:T(8,128)(2,1)S(1)} %get-tuple-element.36), channel_id=1, source_target_pairs={{0,1},{1,5},{2,0},{3,4},{4,3},{5,7},{6,2},{7,6},{8,9},{9,13},{10,8... | collective-permute-start | bytes 1769480 | tf_op jit(solution)/shard_map/ppermute | solution.py:466
  144.6 38.1 %collective-permute-start.22 = (bf16[384,768]{1,0:T(8,128)(2,1)S(1)}, bf16[384,768]{1,0:T(8,128)(2,1)S(1)}, u32[]{:S(2)}, u32[]{:S(2)}) collective-permute-start(bf16[384,768]{1,0:T(8,128)(2,1)S(1)} %shard_map.67), channel_id=1, source_target_pairs={{0,0},{1,4},{2,1},{3,5},{4,2},{5,6},{6,3},{7,7},{8,8},{9,12},{10,9... | collective-permute-start | bytes 1769480 | tf_op jit(solution)/shard_map/ppermute | solution.py:466
  145.4 35.3 %collective-permute-start.19 = (bf16[384,384]{1,0:T(8,128)(2,1)S(1)}, bf16[384,384]{1,0:T(8,128)(2,1)S(1)}, u32[]{:S(2)}, u32[]{:S(2)}) collective-permute-start(bf16[384,384]{1,0:T(8,128)(2,1)S(1)} %get-tuple-element.53), channel_id=1, source_target_pairs={{0,1},{2,3},{4,5},{6,7},{8,9},{10,11},{12,13},{14,15},{16,17},{18,... | collective-permute-start | bytes 884744 | tf_op jit(solution)/shard_map/ppermute | solution.py:481
  163.1 3.4 %collective-permute-start.20 = (bf16[768,128]{1,0:T(8,128)(2,1)S(1)}, bf16[768,128]{1,0:T(8,128)(2,1)S(1)}, u32[]{:S(2)}, u32[]{:S(2)}) collective-permute-start(bf16[768,128]{1,0:T(8,128)(2,1)S(1)} %get-tuple-element.33), channel_id=1, source_target_pairs={{0,0},{1,4},{2,1},{3,5},{4,2},{5,6},{6,3},{7,7},{8,8},{9,12},{10,9... | collective-permute-start | bytes 589832 | tf_op jit(solution)/shard_map/ppermute | solution.py:466
  163.8 17.0 %collective-permute-start.21 = (bf16[768,128]{1,0:T(8,128)(2,1)S(1)}, bf16[768,128]{1,0:T(8,128)(2,1)S(1)}, u32[]{:S(2)}, u32[]{:S(2)}) collective-permute-start(bf16[768,128]{1,0:T(8,128)(2,1)S(1)} %get-tuple-element.34), channel_id=1, source_target_pairs={{0,1},{1,5},{2,0},{3,4},{4,3},{5,7},{6,2},{7,6},{8,9},{9,13},{10,8... | collective-permute-start | bytes 589832 | tf_op jit(solution)/shard_map/ppermute | solution.py:466
